TPU v7x, 32 devices: a whole 2x2x4 slice. The times are simulated.
32 devices in a mesh: row: 4 (over y, core), col: 8 (over z, x).
Axes of the slice: x: 2, y: 2, z: 4, core: 2. Of those that a mesh axis runs over, the one named last changes fastest.
Arguments:
- current_left: bfloat16 [4, 128, 768, 128], P('row', 'col'), may hold values from -6 to 6
- current_right: bfloat16 [4, 128, 768, 128], P('row', 'col'), may hold values from -0.21875 to 0.21875
- current_rank: int32 [4, 128], P('row', 'col'), may hold values from 1 to 128
- target_rank: int32 [4, 128], P('row', 'col'), may hold values from 1 to 128
- update_left: bfloat16 [4, 64, 768, 128], P('row', 'col'), may hold values from -6 to 6
- update_right: bfloat16 [4, 64, 768, 128], P('row', 'col'), may hold values from -0.21875 to 0.21875
- update_rank: int32 [4, 64], P('row', 'col'), may hold values from 1 to 128
- owner_slot: int32 [4, 64], P('row', 'col'), may hold values from 0 to 127, as said below
Outputs:
- compressed_left: bfloat16 [4, 128, 768, 128], P('row', 'col')
- returned_right: bfloat16 [4, 64, 768, 128], P('row', 'col')
- row_scale: float32 [8, 768], P('row')
Inputs may be any that keep to these rules, and one draw needn't show every extreme that they name: `owner_slot`: an entry is the tile's owning column index times 16 plus the tile's place on that owner. No tile is named by two contributions of its grid row. One device names either none or exactly 2 tiles of each owner. In every grid row some owner has all of its 16 tiles named.
All inputs are finite; a program needn't handle non-finite values.
Results may differ from a plain program's by a relative error of at most 0.0085.
Values may be sent and summed in bfloat16 or wider, within the bound.
A program may use at most 128 MiB of HBM per device.

v0:
```python
import math

import jax
import jax.numpy as jnp
from jax import lax
from jax.sharding import PartitionSpec as P

CAP = 2
BR = 2
SWEEPS = 8
ROOTS = 3


def high_dot(first, second):
    return jnp.dot(first, second, precision=lax.Precision.HIGHEST)


def gram_of(stacked):
    return lax.dot_general(
        stacked, stacked, (((0,), (0,)), ((), ())), preferred_element_type=jnp.float32
    )


def split_product(stacked, small):
    upper_part = small.astype(jnp.bfloat16)
    lower_part = (small - upper_part.astype(jnp.float32)).astype(jnp.bfloat16)
    first = jnp.dot(stacked, upper_part, preferred_element_type=jnp.float32)
    return first + jnp.dot(stacked, lower_part, preferred_element_type=jnp.float32)


def square_roots(gram):
    order = gram.shape[0]
    identity = jnp.eye(order, dtype=jnp.float32)
    scale_value = jnp.sqrt(jnp.sum(gram * gram))
    root_now = gram / scale_value
    inverse_now = identity
    for repeat in range(ROOTS):
        middle = 1.5 * identity - 0.5 * high_dot(inverse_now, root_now)
        root_now = high_dot(root_now, middle)
        inverse_now = high_dot(middle, inverse_now)
    return (root_now * jnp.sqrt(scale_value), inverse_now / jnp.sqrt(scale_value))


def recompress(old_left, old_right, old_rank, add_left, add_right, add_rank, keep_rank):
    half_width = old_left.shape[1]
    column = jnp.arange(2 * half_width)
    live_mask = jnp.where(
        column < half_width, column < old_rank, column - half_width < add_rank
    ).astype(jnp.float32)
    live_narrow = live_mask.astype(jnp.bfloat16)
    stack_left = jnp.concatenate([old_left, add_left], axis=1) * live_narrow
    stack_right = jnp.concatenate([old_right, add_right], axis=1) * live_narrow
    gram_left = gram_of(stack_left)
    gram_right = gram_of(stack_right) + jnp.diag(1.0 - live_mask)
    root_factor, inverse_factor = square_roots(gram_right)
    core_matrix = high_dot(high_dot(root_factor, gram_left), root_factor)
    subspace = core_matrix[:, :half_width] + core_matrix[:, half_width:]
    subspace = subspace / jnp.sqrt(jnp.sum(subspace * subspace) + 1e-06)
    for repeat in range(SWEEPS):
        inner = high_dot(subspace.T, subspace)
        subspace = 1.5 * subspace - 0.5 * high_dot(subspace, inner)
    subspace_kept = subspace * (jnp.arange(half_width) < keep_rank).astype(jnp.float32)
    new_left = split_product(stack_left, high_dot(root_factor, subspace_kept))
    solved = high_dot(inverse_factor, subspace_kept)
    new_right = split_product(stack_right, solved) * math.sqrt(stack_right.shape[0])
    return (new_left.astype(jnp.bfloat16), new_right.astype(jnp.bfloat16))


def route_table(owner_slot, tile_count, peer_count):
    destination = owner_slot // tile_count
    local_tile = owner_slot % tile_count
    slot_order = jnp.arange(owner_slot.shape[0])
    same_owner = (destination[:, None] == destination[None, :]) & (
        slot_order[None, :] < slot_order[:, None]
    )
    buffer_place = destination * CAP + jnp.sum(same_owner.astype(jnp.int32), axis=1)
    positions = jnp.arange(peer_count * CAP)
    chosen = buffer_place[None, :] == positions[:, None]
    filled = jnp.any(chosen, axis=1)
    source_slot = jnp.sum(jnp.where(chosen, slot_order[None, :], 0), axis=1)
    return (local_tile, buffer_place, filled, source_slot)


def pack_rows(values, filled, source_slot, peer_count):
    picked = jnp.take(values, source_slot, axis=0)
    shaped_mask = filled.reshape((-1,) + (1,) * (values.ndim - 1))
    packed = jnp.where(shaped_mask, picked, jnp.zeros((), values.dtype))
    return packed.reshape((peer_count, CAP) + values.shape[1:])


def match_tiles(arrived_tile, tile_count):
    matched = arrived_tile[None, :] == jnp.arange(tile_count)[:, None]
    tile_hit = jnp.any(matched, axis=1)
    arrival_index = jnp.sum(
        jnp.where(matched, jnp.arange(arrived_tile.shape[0])[None, :], 0), axis=1
    )
    return (tile_hit, arrival_index)


def flatten_peers(values):
    return values.reshape((values.shape[0] * values.shape[1],) + values.shape[2:])


def local(
    current_left,
    current_right,
    current_rank,
    target_rank,
    update_left,
    update_right,
    update_rank,
    owner_slot,
):
    peer_count = lax.axis_size("col")
    tile_count = current_left.shape[1]
    own_left = current_left[0]
    own_right = current_right[0]
    own_rank = current_rank[0]
    own_target = target_rank[0]
    local_tile, buffer_place, filled, source_slot = route_table(
        owner_slot[0], tile_count, peer_count
    )
    tile_buffer = jnp.where(filled, jnp.take(local_tile, source_slot), tile_count).reshape(
        peer_count, CAP
    )
    keep_cols = jnp.arange(own_left.shape[2]) < own_rank[:, None]
    masked_left = jnp.where(keep_cols[:, None, :], own_left, jnp.zeros((), own_left.dtype))
    asked_tile = flatten_peers(
        lax.all_to_all(tile_buffer, "col", split_axis=0, concat_axis=0, tiled=True)
    )
    asked_used = asked_tile < tile_count
    asked_safe = jnp.minimum(asked_tile, tile_count - 1)
    used_rows = asked_used[:, None, None]
    reply_left = jnp.where(
        used_rows, jnp.take(own_left, asked_safe, axis=0), jnp.zeros((), own_left.dtype)
    )
    reply_right = jnp.where(
        used_rows, jnp.take(own_right, asked_safe, axis=0), jnp.zeros((), own_left.dtype)
    )
    reply_rank = jnp.where(asked_used, jnp.take(own_rank, asked_safe), 0)
    reply_target = jnp.where(asked_used, jnp.take(own_target, asked_safe), 0)
    reply_shape = (peer_count, CAP)
    received = (
        lax.all_to_all(
            reply_left.reshape(reply_shape + own_left.shape[1:]),
            "col",
            split_axis=0,
            concat_axis=0,
            tiled=True,
        ),
        lax.all_to_all(
            reply_right.reshape(reply_shape + own_left.shape[1:]),
            "col",
            split_axis=0,
            concat_axis=0,
            tiled=True,
        ),
        lax.all_to_all(
            reply_rank.reshape(reply_shape), "col", split_axis=0, concat_axis=0, tiled=True
        ),
        lax.all_to_all(
            reply_target.reshape(reply_shape), "col", split_axis=0, concat_axis=0, tiled=True
        ),
    )
    mine_left = jnp.take(flatten_peers(received[0]), buffer_place, axis=0)
    mine_right = jnp.take(flatten_peers(received[1]), buffer_place, axis=0)
    mine_rank = jnp.take(flatten_peers(received[2]), buffer_place)
    mine_target = jnp.take(flatten_peers(received[3]), buffer_place)
    new_left, returned_right = jax.vmap(recompress)(
        mine_left,
        mine_right,
        mine_rank,
        update_left[0],
        update_right[0],
        update_rank[0],
        mine_target,
    )
    send_left = pack_rows(new_left, filled, source_slot, peer_count)
    came_back = flatten_peers(
        lax.all_to_all(send_left, "col", split_axis=0, concat_axis=0, tiled=True)
    )
    tile_hit, arrival_index = match_tiles(asked_tile, tile_count)
    kept_left = jnp.where(
        tile_hit[:, None, None], jnp.take(came_back, arrival_index, axis=0), masked_left
    )
    squares = jnp.sum(jnp.square(kept_left.astype(jnp.float32)), axis=2)
    partial_rows = jnp.sum(squares.reshape(tile_count // BR, BR, squares.shape[1]), axis=0)
    row_sum = lax.psum(partial_rows, "col")
    front_sum = lax.psum(jnp.sum(row_sum), "row")
    mean_value = front_sum / (lax.axis_size("row") * BR * row_sum.shape[1])
    row_scale = jnp.sqrt(row_sum / mean_value)
    return (kept_left[None], returned_right[None], row_scale)


def solution(mesh):
    return jax.shard_map(
        local,
        mesh=mesh,
        in_specs=(
            P("row", "col", None, None),
            P("row", "col", None, None),
            P("row", "col"),
            P("row", "col"),
            P("row", "col", None, None),
            P("row", "col", None, None),
            P("row", "col"),
            P("row", "col"),
        ),
        out_specs=(P("row", "col", None, None), P("row", "col", None, None), P("row", None)),
        check_vma=False,
    )
```

profile of v0, /device:TPU:0, one launch (start us, length us, event | category | flops | bytes accessed | tf_op | source)
XLA Modules:
  0.0 381.6 jit_solution(1778699180939046794)
XLA Ops:
  4.2 13.6 %all_to_all.39 = s32[8,1,2]{2,1,0:T(1,128)S(1)} all-to-all(s32[8,1,2]{2,1,0:T(1,128)S(1)} %bitcast.108), channel_id=1, replica_groups=mesh['row'=4,'col'=8] {'col'}, dimensions={0} | all-to-all | bytes 128 | tf_op jit(solution)/shard_map/all_to_all | solution.py:129
  23.0 3.3 all-to-all-start.2
  26.4 2.6 gather_fusion.6
  29.0 4.7 %gather_fusion.2 = bf16[16,768,128]{2,1,0:T(8,128)(2,1)} fusion(bf16[16,768,128]{2,1,0:T(8,128)(2,1)} %bitcast.104, s32[1024]{0:T(1024)S(1)} %pad_clamp_fusion.2), kind=kCustom, calls=%fused_computation.clone | custom fusion | bytes 6291520 | tf_op jit(solution)/shard_map/jit(_take)/gather | solution.py:135
  33.7 5.9 %all-to-all-start.4 = ((s32[8,1,2]{2,1,0:T(1,128)}), s32[8,1,2]{2,1,0:T(1,128)S(1)}, u32[]{:S(2)}, u32[]{:S(2)}) async-start(s32[8,1,2]{2,1,0:T(1,128)} %bitcast.21), calls=%async_computation.4 | async-start | bytes 8192 | tf_op jit(solution)/shard_map/all_to_all | solution.py:161
  39.6 5.4 %select_select_fusion.1 = (bf16[16,768,128]{2,1,0:T(8,128)(2,1)}, bf16[16,768,128]{2,1,0:T(8,128)(2,1)}) fusion(bf16[16,768,128]{2,1,0:T(8,128)(2,1)S(1)} %copy-done.5, pred[16]{0:T(512)(128)(4,1)S(1)} %get-tuple-element.22, pred[16]{0:T(512)(128)(4,1)S(1)} %get-tuple-element.21, bf16[16,768,128]{2,1,0:T(8,128)(2,1)} %gather_fusion.2), kind=kLoop, calls=%fused_computation.15 | loop fusion | flops 6291456 | bytes 12582944 | tf_op jit(solution)/shard_map/jit(_where)/select_n | solution.py:137
  46.0 73.5 %all_to_all.40 = bf16[8,2,768,128]{3,2,1,0:T(8,128)(2,1)} all-to-all(bf16[8,2,768,128]{3,2,1,0:T(8,128)(2,1)} %bitcast.105), channel_id=1, replica_groups=mesh['row'=4,'col'=8] {'col'}, dimensions={0} | all-to-all | bytes 6291456 | tf_op jit(solution)/shard_map/all_to_all | solution.py:144
  119.5 4.7 %all-to-all-start.3 = ((bf16[8,2,768,128]{3,2,1,0:T(8,128)(2,1)}), bf16[8,2,768,128]{3,2,1,0:T(8,128)(2,1)}, u32[]{:S(2)}, u32[]{:S(2)}) async-start(bf16[8,2,768,128]{3,2,1,0:T(8,128)(2,1)} %bitcast.15), calls=%async_computation.3 | async-start | bytes 6291456 | tf_op jit(solution)/shard_map/all_to_all | solution.py:151
  127.4 2.7 gather_fusion.3
  130.2 63.0 %all-to-all-done.3 = bf16[8,2,768,128]{3,2,1,0:T(8,128)(2,1)} async-done(((bf16[8,2,768,128]{3,2,1,0:T(8,128)(2,1)}), bf16[8,2,768,128]{3,2,1,0:T(8,128)(2,1)}, u32[]{:S(2)}, u32[]{:S(2)}) %all-to-all-start.3) | async-done | bytes 3145760 | tf_op jit(solution)/shard_map/all_to_all | solution.py:151
  193.2 2.7 gather_fusion.7
  201.0 2.5 fusion.2
  206.9 2.5 fusion.7
  254.7 4.0 %gather_fusion.1 = bf16[16,768,128]{2,1,0:T(8,128)(2,1)} fusion(bf16[8,768,128]{2,1,0:T(8,128)(2,1)} %add_convert_fusion, s32[1024]{0:T(1024)S(1)} %pad_clamp_fusion.3), kind=kCustom, calls=%fused_computation.10 | custom fusion | bytes 6291520 | tf_op jit(solution)/shard_map/jit(_take)/gather | solution.py:85
  258.7 4.0 %select_select_fusion.3 = bf16[8,2,768,128]{3,2,1,0:T(8,128)(2,1)} fusion(bf16[8,2,768,128]{3,2,1,0:T(8,128)(2,1)} %bitcast.103, pred[8,2]{1,0:T(8,128)(4,1)S(1)} %compare_and_fusion, pred[8,2]{1,0:T(8,128)(4,1)S(1)} %broadcast_in_dim.177), kind=kLoop, calls=%fused_computation.18 | loop fusion | flops 3145728 | bytes 6291488 | tf_op jit(solution)/shard_map/jit(_where)/select_n | solution.py:87
  262.7 4.8 %all-to-all-start.5 = ((bf16[8,2,768,128]{3,2,1,0:T(8,128)(2,1)}), bf16[8,2,768,128]{3,2,1,0:T(8,128)(2,1)}, u32[]{:S(2)}, u32[]{:S(2)}) async-start(bf16[8,2,768,128]{3,2,1,0:T(8,128)(2,1)} %select_select_fusion.3), calls=%async_computation.5 | async-start | bytes 6291456 | tf_op jit(solution)/shard_map/all_to_all | solution.py:180
  267.9 4.0 %fusion.9 = f32[8,256,256]{2,1,0:T(8,128)S(1)} fusion(f32[8,256,256]{2,1,0:T(8,128)S(1)} %fusion.7, f32[8,256,256]{2,1,0:T(8,128)} %copy-done.3, f32[256,256]{1,0:T(8,128)S(1)} %fusion.52), kind=kOutput, calls=%fused_computation.34 | convolution fusion | flops 1611661312 | bytes 6553600 | tf_op jit(solution)/shard_map/vmap()/dot_general | solution.py:15
  275.1 2.7 fusion.44
  277.8 59.9 %all-to-all-done.5 = bf16[8,2,768,128]{3,2,1,0:T(8,128)(2,1)} async-done(((bf16[8,2,768,128]{3,2,1,0:T(8,128)(2,1)}), bf16[8,2,768,128]{3,2,1,0:T(8,128)(2,1)}, u32[]{:S(2)}, u32[]{:S(2)}) %all-to-all-start.5) | async-done | bytes 3145760 | tf_op jit(solution)/shard_map/all_to_all | solution.py:180
  337.7 4.7 %gather_fusion.10 = bf16[16,768,128]{2,1,0:T(8,128)(2,1)} fusion(bf16[16,768,128]{2,1,0:T(8,128)(2,1)} %bitcast.23, s32[1024]{0:T(1024)S(1)} %pad_clamp_fusion), kind=kCustom, calls=%fused_computation.5.clone | custom fusion | bytes 6291520 | tf_op jit(solution)/shard_map/jit(_take)/gather | solution.py:184
  342.4 5.3 %multiply_reduce_fusion = (f32[16,768]{1,0:T(8,128)S(1)}, bf16[16,768,128]{2,1,0:T(8,128)(2,1)}) fusion(bf16[1,16,768,128]{3,2,1,0:T(8,128)(2,1)S(1)} %copy-done.4, pred[16,128]{1,0:T(8,128)(4,1)S(1)} %iota_compare_fusion.3, bf16[16,768,128]{2,1,0:T(8,128)(2,1)} %gather_fusion.10, pred[16]{0:T(512)(128)(4,1)S(1)} %compare_and_fusion.1, ...), kind=kLoop, calls=%fused_computation.11 | loop fusion | flops 9424896 | bytes 9488416 | tf_op jit(solution)/shard_map/reduce_sum | solution.py:186
  347.7 19.7 %psum.14 = f32[2,768]{1,0:T(2,128)S(1)} all-reduce(f32[2,768]{1,0:T(2,128)S(1)} %reduce_sum.90), channel_id=1, replica_groups=mesh['row'=4,'col'=8] {'col'}, use_global_device_ids=true, to_apply=%region_9.14 | all-reduce | flops 1536 | bytes 12288 | tf_op jit(solution)/shard_map/psum | solution.py:188
  368.1 5.8 %fusion.17 = bf16[1,8,768,128]{3,2,1,0:T(8,128)(2,1)} fusion(f32[8,768,128]{2,1,0:T(8,128)} %fusion.44, f32[8,256,128]{2,1,0:T(8,128)} %copy-done.14, bf16[8,768,128]{2,1,0:T(8,128)(2,1)} %bitcast.114, bf16[8,768,128]{2,1,0:T(8,128)(2,1)} %copy-done.8, bf16[8,256]{1,0:T(8,128)(2,1)S(1)} %convert_convert_fusion), kind=kOutput, calls=%fused_computation.44 | convolution fusion | flops 415498240 | bytes 8916992 | tf_op jit(solution)/shard_map/vmap()/dot_general | solution.py:28
  373.8 6.3 %psum.15 = f32[]{:T(128)} all-reduce(f32[]{:T(128)} %reduce_sum.91), channel_id=1, replica_groups=mesh['row'=4,'col'=8] {'row'}, use_global_device_ids=true, to_apply=%region_11.16 | all-reduce | flops 1 | bytes 8 | tf_op jit(solution)/shard_map/psum | solution.py:189
  (119 shorter events, 71.2 us)
Async XLA Ops:
  0.6 25.7 %copy-start = (bf16[1,16,768,128]{3,2,1,0:T(8,128)(2,1)S(1)}, bf16[1,16,768,128]{3,2,1,0:T(8,128)(2,1)}, u32[]{:S(2)}) copy-start(bf16[1,16,768,128]{3,2,1,0:T(8,128)(2,1)} %param.17) | copy-start | bytes 9437188
  23.0 10.6 %all-to-all-start.2 = ((s32[8,1,2]{2,1,0:T(1,128)}), s32[8,1,2]{2,1,0:T(1,128)S(1)}, u32[]{:S(2)}, u32[]{:S(2)}) async-start(s32[8,1,2]{2,1,0:T(1,128)} %bitcast.12), calls=%async_computation.2 | async-start | bytes 8192 | tf_op jit(solution)/shard_map/all_to_all | solution.py:158
  29.0 10.6 %copy-start.5 = (bf16[16,768,128]{2,1,0:T(8,128)(2,1)S(1)}, bf16[16,768,128]{2,1,0:T(8,128)(2,1)}, u32[]{:S(2)}) copy-start(bf16[16,768,128]{2,1,0:T(8,128)(2,1)} %gather_fusion.6) | copy-start | bytes 9437188
  33.7 12.3 %all-to-all-start.4 = ((s32[8,1,2]{2,1,0:T(1,128)}), s32[8,1,2]{2,1,0:T(1,128)S(1)}, u32[]{:S(2)}, u32[]{:S(2)}) async-start(s32[8,1,2]{2,1,0:T(1,128)} %bitcast.21), calls=%async_computation.4 | async-start | bytes 8192 | tf_op jit(solution)/shard_map/all_to_all | solution.py:161
  119.5 7.8 %copy-start.10 = (s32[1,8]{1,0:T(1,128)S(1)}, s32[1,8]{1,0:T(1,128)}, u32[]{:S(2)}) copy-start(s32[1,8]{1,0:T(1,128)} %param.22) | copy-start | bytes 100
  119.5 73.7 %all-to-all-start.3 = ((bf16[8,2,768,128]{3,2,1,0:T(8,128)(2,1)}), bf16[8,2,768,128]{3,2,1,0:T(8,128)(2,1)}, u32[]{:S(2)}, u32[]{:S(2)}) async-start(bf16[8,2,768,128]{3,2,1,0:T(8,128)(2,1)} %bitcast.15), calls=%async_computation.3 | async-start | bytes 6291456 | tf_op jit(solution)/shard_map/all_to_all | solution.py:151
  196.0 1.6 copy-start.12
  196.3 3.1 copy-start.8
  213.9 2.3 copy-start.3
  213.9 2.3 copy-start.11
  248.4 1.0 copy-start.6
  262.7 4.8 %copy-start.2 = (s32[1,16]{1,0:T(1,128)S(1)}, s32[1,16]{1,0:T(1,128)}, u32[]{:S(2)}) copy-start(s32[1,16]{1,0:T(1,128)} %param.18) | copy-start | bytes 196
  262.7 75.0 %all-to-all-start.5 = ((bf16[8,2,768,128]{3,2,1,0:T(8,128)(2,1)}), bf16[8,2,768,128]{3,2,1,0:T(8,128)(2,1)}, u32[]{:S(2)}, u32[]{:S(2)}) async-start(bf16[8,2,768,128]{3,2,1,0:T(8,128)(2,1)} %select_select_fusion.3), calls=%async_computation.5 | async-start | bytes 6291456 | tf_op jit(solution)/shard_map/all_to_all | solution.py:180
  267.9 4.0 %copy-start.7 = (f32[8,256,128]{2,1,0:T(8,128)S(1)}, f32[8,256,128]{2,1,0:T(8,128)}, u32[]{:S(2)}) copy-start(f32[8,256,128]{2,1,0:T(8,128)} %copy-done.6) | copy-start | bytes 3145732
  271.9 3.2 copy-start.9
  271.9 3.2 copy-start.13
  274.0 1.1 copy-start.14
  337.7 4.7 %copy-start.4 = (bf16[1,16,768,128]{3,2,1,0:T(8,128)(2,1)S(1)}, bf16[1,16,768,128]{3,2,1,0:T(8,128)(2,1)}, u32[]{:S(2)}) copy-start(bf16[1,16,768,128]{3,2,1,0:T(8,128)(2,1)} %param.16) | copy-start | bytes 9437188
  368.1 13.3 %copy-start.1 = (bf16[1,16,768,128]{3,2,1,0:T(8,128)(2,1)S(1)}, bf16[1,16,768,128]{3,2,1,0:T(8,128)(2,1)}, u32[]{:S(2)}) copy-start(bf16[1,16,768,128]{3,2,1,0:T(8,128)(2,1)} %param.17) | copy-start | bytes 9437188
where the time goes:
time: 385 us; the launch traced here: 382 us
  waiting for transfers between devices  124 us (32%)
  blocking collectives  113 us (29%)
  matrix products  70.1 us (18%)
  local copies, waits for them, and re-layouts  32 us (8%)
  other arithmetic  21.6 us (6%)
  starting transfers between devices  18.8 us (5%)
    all_to_all x1, blocking collectives, local(): lax.all_to_all(reply_left.reshape(reply_shape + own_left.shape[1:]), 'col...  73.5 us
    all_to_all x1, waiting for transfers between devices, local(): lax.all_to_all(reply_right.reshape(reply_shape + own_left.shape[1:]), 'co...  63 us
    all_to_all x1, waiting for transfers between devices, local(): lax.all_to_all(send_left, 'col', split_axis=0, concat_axis=0, tiled=True)  59.9 us
    dot_general x29, matrix products, high_dot(): return jnp.dot(first, second, precision=lax.Precision.HIGHEST)  54.2 us
    psum x1, blocking collectives, local(): row_sum = lax.psum(partial_rows, 'col')  19.7 us
    all_to_all x1, blocking collectives, local(): lax.all_to_all(tile_buffer, 'col', split_axis=0, concat_axis=0, tiled=True)  13.6 us
    dot_general x2, matrix products, split_product(): jnp.dot(stacked, lower_part, preferred_element_type=jnp.float32)  7.95 us
  transfers between devices with their start and end apart: 4, of which 3 were waited for; matrix products, arithmetic and copies ran while one was open for 7% of the time, Pallas kernels for 0%

commit v1 on v0

v1 whole, which is shorter than its diff:
```python
import functools
import math

import jax
import jax.numpy as jnp
from jax import lax
from jax.experimental import pallas as pl
from jax.experimental.pallas import tpu as pltpu
from jax.sharding import PartitionSpec as P

CAP = 2
BR = 2
SWEEPS = 8
ROOTS = 3
F32 = jnp.float32
BF16 = jnp.bfloat16
HIGH = lax.Precision.HIGH


def bmm(a, b):
    return jnp.einsum("bij,bjk->bik", a, b, precision=HIGH, preferred_element_type=F32)


def contract_rows(a, b):
    return lax.dot_general(a, b, (((0,), (0,)), ((), ())), preferred_element_type=F32)


def gather_kernel(n, x_ref, o_ref, send_sem, recv_sem, own_sem):
    row, me = lax.axis_index("row"), lax.axis_index("col")
    barrier = pltpu.get_barrier_semaphore()
    for step in range(1, n):
        peer = lax.rem(me + step, n)
        pl.semaphore_signal(
            barrier, inc=1, device_id=(row, peer), device_id_type=pl.DeviceIdType.MESH
        )
    pl.semaphore_wait(barrier, n - 1)
    own = pltpu.make_async_copy(x_ref, o_ref.at[me], own_sem)
    own.start()
    copies = []
    for step in range(1, n):
        peer = lax.rem(me + step, n)
        copy = pltpu.make_async_remote_copy(
            src_ref=x_ref,
            dst_ref=o_ref.at[me],
            send_sem=send_sem.at[step],
            recv_sem=recv_sem.at[step],
            device_id=(row, peer),
            device_id_type=pl.DeviceIdType.MESH,
        )
        copy.start()
        copies.append(copy)
    own.wait()
    for copy in copies:
        copy.wait()


def gather_small(x, n):
    return pl.pallas_call(
        functools.partial(gather_kernel, n),
        out_shape=jax.ShapeDtypeStruct((n,) + x.shape, x.dtype),
        in_specs=[pl.BlockSpec(memory_space=pltpu.VMEM)],
        out_specs=pl.BlockSpec(memory_space=pltpu.VMEM),
        scratch_shapes=[
            pltpu.SemaphoreType.DMA((n,)),
            pltpu.SemaphoreType.DMA((n,)),
            pltpu.SemaphoreType.DMA,
        ],
        compiler_params=pltpu.CompilerParams(collective_id=0, has_side_effects=True),
        name="gather_small",
    )(x)


def scale_kernel(n, m, x_ref, o_ref, parts, mine, totals, sems, own_sem):
    send_a, recv_a, send_b, recv_b = (sems.at[i] for i in range(4))
    row, me = lax.axis_index("row"), lax.axis_index("col")
    barrier = pltpu.get_barrier_semaphore()
    for step in range(1, n):
        pl.semaphore_signal(
            barrier,
            inc=1,
            device_id=(row, lax.rem(me + step, n)),
            device_id_type=pl.DeviceIdType.MESH,
        )
    for step in range(1, m):
        pl.semaphore_signal(
            barrier,
            inc=1,
            device_id=(lax.rem(row + step, m), me),
            device_id_type=pl.DeviceIdType.MESH,
        )
    pl.semaphore_wait(barrier, n + m - 2)
    copies = []
    for step in range(1, n):
        copy = pltpu.make_async_remote_copy(
            src_ref=x_ref,
            dst_ref=parts.at[me],
            send_sem=send_a.at[step],
            recv_sem=recv_a.at[step],
            device_id=(row, lax.rem(me + step, n)),
            device_id_type=pl.DeviceIdType.MESH,
        )
        copy.start()
        copies.append(copy)
    own = pltpu.make_async_copy(x_ref, parts.at[me], own_sem.at[0])
    own.start()
    own.wait()
    for copy in copies:
        copy.wait()
    row_sum = jnp.sum(parts[...], axis=0)
    total = jnp.sum(jnp.sum(row_sum, axis=1, keepdims=True), axis=0, keepdims=True)
    mine[0] = jnp.broadcast_to(total, mine.shape[1:])
    fill = pltpu.make_async_copy(mine.at[0], mine.at[1], own_sem.at[1])
    fill.start()
    fill.wait()
    copies = []
    for step in range(1, m):
        copy = pltpu.make_async_remote_copy(
            src_ref=mine.at[1],
            dst_ref=totals.at[row],
            send_sem=send_b.at[step],
            recv_sem=recv_b.at[step],
            device_id=(lax.rem(row + step, m), me),
            device_id_type=pl.DeviceIdType.MESH,
        )
        copy.start()
        copies.append(copy)
    own = pltpu.make_async_copy(mine.at[1], totals.at[row], own_sem.at[0])
    own.start()
    own.wait()
    for copy in copies:
        copy.wait()
    everything = jnp.sum(totals[...], axis=0)[:1, :1]
    count = m * x_ref.shape[0] * x_ref.shape[1]
    o_ref[...] = jnp.sqrt(row_sum / (everything * (1.0 / count)))


def scale_rows(x, n, m):
    width = max(n, m)
    return pl.pallas_call(
        functools.partial(scale_kernel, n, m),
        out_shape=jax.ShapeDtypeStruct(x.shape, F32),
        in_specs=[pl.BlockSpec(memory_space=pltpu.VMEM)],
        out_specs=pl.BlockSpec(memory_space=pltpu.VMEM),
        scratch_shapes=[
            pltpu.VMEM((n,) + x.shape, F32),
            pltpu.VMEM((2, 8, 128), F32),
            pltpu.VMEM((m, 8, 128), F32),
            pltpu.SemaphoreType.DMA((4, width)),
            pltpu.SemaphoreType.DMA((2,)),
        ],
        compiler_params=pltpu.CompilerParams(collective_id=1, has_side_effects=True),
        name="scale_rows",
    )(x)


def owner_gram_kernel(tile_ref, cur_ref, upd_ref, o_ref):
    half = cur_ref.shape[1]
    o_ref[:, :half] = contract_rows(cur_ref[...], cur_ref[...]).astype(BF16)
    o_ref[:, half:] = contract_rows(cur_ref[...], upd_ref[...]).astype(BF16)


def owner_gram(asked, current, arrived):
    slots, order, half = arrived.shape
    return pl.pallas_call(
        owner_gram_kernel,
        grid_spec=pltpu.PrefetchScalarGridSpec(
            num_scalar_prefetch=1,
            grid=(slots,),
            in_specs=[
                pl.BlockSpec((None, order, half), lambda s, t: (t[s], 0, 0)),
                pl.BlockSpec((None, order, half), lambda s, t: (s, 0, 0)),
            ],
            out_specs=pl.BlockSpec((None, half, 2 * half), lambda s, t: (s, 0, 0)),
        ),
        out_shape=jax.ShapeDtypeStruct((slots, half, 2 * half), BF16),
        name="owner_gram",
    )(asked, current, arrived)


def owner_left_kernel(from_ref, hit_ref, rank_ref, cur_ref, upd_ref, mix_ref, o_ref, sum_ref):
    t = pl.program_id(0)
    half = cur_ref.shape[1]

    @pl.when(t == 0)
    def _():
        sum_ref[...] = jnp.zeros_like(sum_ref)

    @pl.when(hit_ref[t] > 0)
    def _():
        fresh = jnp.dot(cur_ref[...], mix_ref[:half], preferred_element_type=F32)
        fresh += jnp.dot(upd_ref[...], mix_ref[half:], preferred_element_type=F32)
        o_ref[...] = fresh.astype(BF16)

    @pl.when(hit_ref[t] == 0)
    def _():
        column = lax.broadcasted_iota(jnp.int32, cur_ref.shape, 1)
        o_ref[...] = jnp.where(
            column < rank_ref[t], cur_ref[...].astype(F32), 0.0
        ).astype(BF16)

    kept = o_ref[...].astype(F32)
    sums = lax.dot_general(
        jnp.ones((8, half), F32),
        kept * kept,
        (((1,), (1,)), ((), ())),
        precision=lax.Precision.HIGHEST,
        preferred_element_type=F32,
    )
    which = lax.broadcasted_iota(jnp.int32, sum_ref.shape, 0)
    sum_ref[...] += jnp.where(which == t % BR, sums[:BR], 0.0)


def owner_left(arrival, hit, rank, current, arrived, mix):
    tiles, order, half = current.shape
    return pl.pallas_call(
        owner_left_kernel,
        grid_spec=pltpu.PrefetchScalarGridSpec(
            num_scalar_prefetch=3,
            grid=(tiles,),
            in_specs=[
                pl.BlockSpec((None, order, half), lambda t, f, h, r: (t, 0, 0)),
                pl.BlockSpec((None, order, half), lambda t, f, h, r: (f[t], 0, 0)),
                pl.BlockSpec((None, 2 * half, half), lambda t, f, h, r: (f[t], 0, 0)),
            ],
            out_specs=[
                pl.BlockSpec((None, order, half), lambda t, f, h, r: (t, 0, 0)),
                pl.BlockSpec((BR, order), lambda t, f, h, r: (0, 0)),
            ],
        ),
        out_shape=[
            jax.ShapeDtypeStruct((tiles, order, half), BF16),
            jax.ShapeDtypeStruct((BR, order), F32),
        ],
        name="owner_left",
    )(arrival, hit, rank, current, arrived, mix)


def right_kernel(place_ref, cur_ref, upd_ref, mix_ref, o_ref):
    half = cur_ref.shape[1]
    fresh = jnp.dot(cur_ref[...], mix_ref[:half], preferred_element_type=F32)
    fresh += jnp.dot(upd_ref[...], mix_ref[half:], preferred_element_type=F32)
    o_ref[...] = fresh.astype(BF16)


def right_out(place, received, update, mix):
    slots, order, half = update.shape
    return pl.pallas_call(
        right_kernel,
        grid_spec=pltpu.PrefetchScalarGridSpec(
            num_scalar_prefetch=1,
            grid=(slots,),
            in_specs=[
                pl.BlockSpec((None, order, half), lambda j, p: (p[j], 0, 0)),
                pl.BlockSpec((None, order, half), lambda j, p: (j, 0, 0)),
                pl.BlockSpec((None, 2 * half, half), lambda j, p: (j, 0, 0)),
            ],
            out_specs=pl.BlockSpec((None, order, half), lambda j, p: (j, 0, 0)),
        ),
        out_shape=jax.ShapeDtypeStruct((slots, order, half), BF16),
        cost_estimate=pl.CostEstimate(
            flops=4 * slots * order * half * half,
            bytes_accessed=6 * slots * order * half,
            transcendentals=0,
        ),
        name="right_out",
    )(place, received, update, mix)


def right_gram_kernel(place_ref, cur_ref, upd_ref, o_ref):
    half = cur_ref.shape[1]
    cross = contract_rows(cur_ref[...], upd_ref[...])
    o_ref[:half, :half] = contract_rows(cur_ref[...], cur_ref[...])
    o_ref[:half, half:] = cross
    o_ref[half:, :half] = cross.T
    o_ref[half:, half:] = contract_rows(upd_ref[...], upd_ref[...])


def right_gram(place, received, update):
    slots, order, half = update.shape
    return pl.pallas_call(
        right_gram_kernel,
        grid_spec=pltpu.PrefetchScalarGridSpec(
            num_scalar_prefetch=1,
            grid=(slots,),
            in_specs=[
                pl.BlockSpec((None, order, half), lambda j, p: (p[j], 0, 0)),
                pl.BlockSpec((None, order, half), lambda j, p: (j, 0, 0)),
            ],
            out_specs=pl.BlockSpec((None, 2 * half, 2 * half), lambda j, p: (j, 0, 0)),
        ),
        out_shape=jax.ShapeDtypeStruct((slots, 2 * half, 2 * half), F32),
        name="right_gram",
    )(place, received, update)


def swap(values, n):
    shaped = values.reshape((n, CAP) + values.shape[1:])
    out = lax.all_to_all(shaped, "col", split_axis=0, concat_axis=0, tiled=True)
    return out.reshape(values.shape)


def take(values, index):
    return jnp.take(values, index, axis=0, mode="clip")


def local(
    current_left,
    current_right,
    current_rank,
    target_rank,
    update_left,
    update_right,
    update_rank,
    owner_slot,
):
    n = lax.axis_size("col")
    m = lax.axis_size("row")
    me = lax.axis_index("col")
    own_left, own_right = current_left[0], current_right[0]
    add_left, add_right = update_left[0], update_right[0]
    tiles, order, half = own_left.shape
    slots = owner_slot.shape[1]
    slot_index = jnp.arange(slots)

    mine = owner_slot[0]
    owner = mine // tiles
    earlier = (owner[:, None] == owner[None, :]) & (slot_index[None, :] < slot_index[:, None])
    place = owner * CAP + jnp.sum(earlier.astype(jnp.int32), axis=1)
    chosen = place[None, :] == jnp.arange(n * CAP)[:, None]
    source = jnp.sum(jnp.where(chosen, slot_index[None, :], 0), axis=1)
    arrived_left = swap(take(add_left, source), n)

    packed = jnp.concatenate([mine, current_rank[0], target_rank[0]])
    width = -(-packed.shape[0] // 128) * 128
    packed = jnp.pad(packed, (0, width - packed.shape[0])).reshape(1, width)
    table = gather_small(packed, n)[:, 0, :]
    named = table[:, :slots]
    ranks = table[:, slots : slots + tiles].reshape(-1)
    targets = table[:, slots + tiles : slots + 2 * tiles].reshape(-1)
    my_rank = jnp.sum(
        jnp.where(mine[:, None] == jnp.arange(n * tiles)[None, :], ranks[None, :], 0), axis=1
    )
    my_target = jnp.sum(
        jnp.where(mine[:, None] == jnp.arange(n * tiles)[None, :], targets[None, :], 0), axis=1
    )
    to_me = (named // tiles) == me
    count = jnp.sum(
        (to_me[:, None, :] & (slot_index[None, None, :] < slot_index[None, :, None])).astype(
            jnp.int32
        ),
        axis=2,
    )
    picked = to_me[:, None, :] & (count[:, None, :] == jnp.arange(CAP)[None, :, None])
    asked = jnp.sum(jnp.where(picked, (named % tiles)[:, None, :], 0), axis=2).reshape(-1)
    asked_used = jnp.any(picked, axis=2).reshape(-1)

    received_right = swap(take(own_right, asked), n)
    grams = swap(owner_gram(asked, own_left, arrived_left), n)

    column = jnp.arange(2 * half)[None, :]
    live = jnp.where(
        column < half, column < my_rank[:, None], column - half < update_rank[0][:, None]
    ).astype(F32)
    both = live[:, :, None] * live[:, None, :]
    identity = jnp.eye(2 * half, dtype=F32)
    gram_right = right_gram(place, received_right, add_right) * both
    gram_right = gram_right + identity * (1.0 - live)[:, :, None]
    c = jnp.sqrt(jnp.sum(gram_right * gram_right, axis=(1, 2), keepdims=True))
    root = gram_right / c
    inverse = 1.5 * identity - 0.5 * root
    root = bmm(root, inverse)
    for _ in range(ROOTS - 1):
        middle = 1.5 * identity - 0.5 * bmm(inverse, root)
        root = bmm(root, middle)
        inverse = bmm(middle, inverse)
    root = root * jnp.sqrt(c)
    inverse = inverse * lax.rsqrt(c)

    own_gram = jnp.einsum("bki,bkj->bij", add_left, add_left, preferred_element_type=F32)
    top = take(grams, place).astype(F32)
    low = jnp.concatenate([jnp.swapaxes(top[:, :, half:], 1, 2), own_gram], axis=2)
    gram_left = jnp.concatenate([top, low], axis=1) * both
    core = bmm(root, gram_left)
    core = bmm(core, root[:, :, :half] + root[:, :, half:])
    y = core * lax.rsqrt(jnp.sum(core * core, axis=(1, 2), keepdims=True) + 1e-06)
    for _ in range(SWEEPS):
        inner = jnp.einsum("bki,bkj->bij", y, y, precision=HIGH, preferred_element_type=F32)
        y = 1.5 * y - 0.5 * bmm(y, inner)
    y = y * (jnp.arange(half)[None, :] < my_target[:, None]).astype(F32)[:, None, :]
    mix_left = (bmm(root, y) * live[:, :, None]).astype(BF16)
    mix_right = (bmm(inverse, y) * (live[:, :, None] * math.sqrt(order))).astype(BF16)

    arrived_mix = swap(take(mix_left, source), n)
    returned_right = right_out(place, received_right, add_right, mix_right)

    matched = (asked[None, :] == jnp.arange(tiles)[:, None]) & asked_used[None, :]
    hit = jnp.any(matched, axis=1).astype(jnp.int32)
    arrival = jnp.sum(
        jnp.where(matched, jnp.arange(n * CAP)[None, :], 0), axis=1
    ).astype(jnp.int32)
    kept, partial = owner_left(
        arrival, hit, current_rank[0], own_left, arrived_left, arrived_mix
    )
    return (kept[None], returned_right[None], scale_rows(partial, n, m))


def solution(mesh):
    return jax.shard_map(
        local,
        mesh=mesh,
        in_specs=(
            P("row", "col", None, None),
            P("row", "col", None, None),
            P("row", "col"),
            P("row", "col"),
            P("row", "col", None, None),
            P("row", "col", None, None),
            P("row", "col"),
            P("row", "col"),
        ),
        out_specs=(P("row", "col", None, None), P("row", "col", None, None), P("row", None)),
        check_vma=False,
    )
```

time: 385 us -> 296 us (0.77)
  blocking collectives: 113 us -> 0 us
  Pallas kernels: 0 us -> 65.3 us
  matrix products: 70.1 us -> 36.5 us
  waiting for transfers between devices: 124 us -> 146 us
  other arithmetic: 21.6 us -> 7.74 us
  local copies, waits for them, and re-layouts: 32 us -> 20 us
    all_to_all x2 -> x0, blocking collectives: 87.1 us -> none  [the longest x1 73.5 us: local(): lax.all_to_all(reply_left.reshape(reply_shape + own_left.shape[1:]), 'col...]
    pallas_call x0 -> x6, Pallas kernels: none -> 65.3 us  [the longest x1 15.7 us: owner_left(): pl.pallas_call(owner_left_kernel, grid_spec=pltpu.PrefetchScalarGridSpec(...]
    dot_general x35 -> x28, matrix products: 70.1 us -> 36.5 us  [the longest x19 24.7 us: bmm(): jnp.einsum('bij,bjk->bik', a, b, precision=HIGH, preferred_element_type=F32)]
    psum x2 -> x0, blocking collectives: 26 us -> none  [the longest x1 19.7 us: local(): row_sum = lax.psum(partial_rows, 'col')]
    all_to_all x4, waiting for transfers between devices: 124 us -> 146 us  [swap(): out = lax.all_to_all(shaped, 'col', split_axis=0, concat_axis=0, tiled=True)]
    gather x12 -> x5, local copies, waits for them, and re-layouts: 26.1 us -> 11 us  [take(): return jnp.take(values, index, axis=0, mode='clip')]
    select_n x10 -> x2, other arithmetic: 10.5 us -> 0.7 us  [the longest x1 0.69 us: local(): named % tiles]
  transfers between devices with their start and end apart: 4 -> 4, of which waited for: 3 -> 4; matrix products, arithmetic and copies ran while one was open for 7% -> 10% of each run, Pallas kernels for 0% -> 5%
where the time goes in v1:
time: 296 us; the launch traced here: 295 us
  waiting for transfers between devices  146 us (49%)
  Pallas kernels  65.3 us (22%)
  matrix products  36.5 us (12%)
  local copies, waits for them, and re-layouts  20 us (7%)
  starting transfers between devices  18.1 us (6%)
  other arithmetic  7.74 us (3%)
    all_to_all x4, waiting for transfers between devices, swap(): out = lax.all_to_all(shaped, 'col', split_axis=0, concat_axis=0, tiled=True)  146 us
    dot_general x19, matrix products, bmm(): jnp.einsum('bij,bjk->bik', a, b, precision=HIGH, preferred_element_type=F32)  24.7 us
    all_to_all x4, starting transfers between devices, swap(): out = lax.all_to_all(shaped, 'col', split_axis=0, concat_axis=0, tiled=True)  18.1 us
    pallas_call x1, Pallas kernels, owner_left(): pl.pallas_call(owner_left_kernel, grid_spec=pltpu.PrefetchScalarGridSpec(...  15.7 us
    pallas_call x1, Pallas kernels, owner_gram(): pl.pallas_call(owner_gram_kernel, grid_spec=pltpu.PrefetchScalarGridSpec(...  12.8 us
    pallas_call x1, Pallas kernels, scale_rows(): pl.pallas_call(functools.partial(scale_kernel, n, m), out_shape=jax.Shape...  11.8 us
    gather x5, local copies, waits for them, and re-layouts, take(): return jnp.take(values, index, axis=0, mode='clip')  11 us
    pallas_call x1, Pallas kernels, gather_small(): pl.pallas_call(functools.partial(gather_kernel, n), out_shape=jax.ShapeDt...  9.54 us
  transfers between devices with their start and end apart: 4, of which 4 were waited for; matrix products, arithmetic and copies ran while one was open for 10% of the time, Pallas kernels for 5%

profile of v1, /device:TPU:0, one launch (start us, length us, event | category | flops | bytes accessed | tf_op | source)
XLA Modules:
  0.0 294.8 jit_solution(15765337892123221834)
XLA Ops:
  2.1 9.5 %gather_small.1 = s32[8,1,128]{2,1,0:T(1,128)} custom-call(s32[1,128]{1,0:T(1,128)} %pad_bitcast_fusion.x_ref), custom_call_target="tpu_custom_call" | custom-call | tf_op jit(solution)/shard_map/gather_small/pallas_call | solution.py:58
  13.6 2.6 gather_fusion.1
  16.2 5.6 %all-to-all-start.1 = ((bf16[8,2,768,128]{3,2,1,0:T(8,128)(2,1)}), bf16[8,2,768,128]{3,2,1,0:T(8,128)(2,1)S(1)}, u32[]{:S(2)}, u32[]{:S(2)}) async-start(bf16[8,2,768,128]{3,2,1,0:T(8,128)(2,1)} %bitcast.99), calls=%async_computation.1 | async-start | bytes 6291456 | tf_op jit(solution)/shard_map/all_to_all | solution.py:298
  22.1 4.0 %gather_fusion = bf16[16,768,128]{2,1,0:T(8,128)(2,1)} fusion(bf16[8,768,128]{2,1,0:T(8,128)(2,1)} %bitcast.97, s32[1024]{0:T(1024)S(1)} %pad_clamp_fusion.2), kind=kCustom, calls=%fused_computation | custom fusion | bytes 6291520 | tf_op jit(solution)/shard_map/jit(_take)/gather | solution.py:303
  26.1 65.2 %all-to-all-done.1 = bf16[8,2,768,128]{3,2,1,0:T(8,128)(2,1)S(1)} async-done(((bf16[8,2,768,128]{3,2,1,0:T(8,128)(2,1)}), bf16[8,2,768,128]{3,2,1,0:T(8,128)(2,1)S(1)}, u32[]{:S(2)}, u32[]{:S(2)}) %all-to-all-start.1) | async-done | bytes 3145760 | tf_op jit(solution)/shard_map/all_to_all | solution.py:298
  91.3 1.7 copy-done.2
  93.0 4.4 %all-to-all-start = ((bf16[8,2,768,128]{3,2,1,0:T(8,128)(2,1)}), bf16[8,2,768,128]{3,2,1,0:T(8,128)(2,1)}, u32[]{:S(2)}, u32[]{:S(2)}) async-start(bf16[8,2,768,128]{3,2,1,0:T(8,128)(2,1)} %bitcast.98), calls=%async_computation | async-start | bytes 6291456 | tf_op jit(solution)/shard_map/all_to_all | solution.py:298
  98.8 3.4 %fusion.68 = f32[8,128,128]{2,1,0:T(8,128)} fusion(bf16[1,8,768,128]{3,2,1,0:T(8,128)(2,1)} %param.12), kind=kOutput, calls=%fused_computation.133 | convolution fusion | flops 201326592 | bytes 2097152 | tf_op jit(solution)/shard_map/bki,bkj->bij/dot_general | solution.py:379
  102.2 8.0 %right_gram.1 = f32[8,256,256]{2,1,0:T(8,128)} custom-call(s32[8]{0:T(128)} %multiply_add_fusion.place_ref, bf16[16,768,128]{2,1,0:T(8,128)(2,1)} %bitcast.95, bf16[8,768,128]{2,1,0:T(8,128)(2,1)} %bitcast.102), custom_call_target="tpu_custom_call" | custom-call | tf_op jit(solution)/shard_map/right_gram/pallas_call | solution.py:280
  110.2 2.1 multiply_reduce_fusion
  112.3 55.3 %all-to-all-done = bf16[8,2,768,128]{3,2,1,0:T(8,128)(2,1)} async-done(((bf16[8,2,768,128]{3,2,1,0:T(8,128)(2,1)}), bf16[8,2,768,128]{3,2,1,0:T(8,128)(2,1)}, u32[]{:S(2)}, u32[]{:S(2)}) %all-to-all-start) | async-done | bytes 3145760 | tf_op jit(solution)/shard_map/all_to_all | solution.py:298
  167.6 12.8 %owner_gram.1 = bf16[16,128,256]{2,1,0:T(8,128)(2,1)} custom-call(s32[16]{0:T(128)} %copy-done.15, bf16[16,768,128]{2,1,0:T(8,128)(2,1)} %bitcast.100, bf16[16,768,128]{2,1,0:T(8,128)(2,1)} %bitcast.11.upd_ref), custom_call_target="tpu_custom_call" | custom-call | tf_op jit(solution)/shard_map/owner_gram/pallas_call | solution.py:164
  180.4 3.9 %all-to-all-start.2 = ((bf16[8,2,128,256]{3,2,1,0:T(8,128)(2,1)}), bf16[8,2,128,256]{3,2,1,0:T(8,128)(2,1)S(1)}, u32[]{:S(2)}, u32[]{:S(2)}) async-start(bf16[8,2,128,256]{3,2,1,0:T(8,128)(2,1)} %bitcast.105), calls=%async_computation.2 | async-start | bytes 2097152 | tf_op jit(solution)/shard_map/all_to_all | solution.py:298
  184.3 3.1 %fusion.11 = f32[8,256,256]{2,1,0:T(8,128)S(1)} fusion(f32[256,256]{1,0:T(8,128)S(1)} %fusion.52, f32[8,256,256]{2,1,0:T(8,128)S(1)} %copy-done.8, f32[8]{0:T(128)S(1)} %get-tuple-element.17, f32[8,256]{1,0:T(8,128)S(1)} %get-tuple-element.14, f32[256,256]{1,0:T(8,128)} %copy-done.12, f32[8,256]{1,0:T(8,128)S(1)} %fusion.60), kind=kOutput, calls=%fused_computation.20 | convolution fusion | flops 811597824 | bytes 4735008 | tf_op jit(solution)/shard_map/bij,bjk->bik/dot_general | solution.py:21
  187.4 1.9 multiply_subtract_fusion.1
  196.4 14.0 %all-to-all-done.2 = bf16[8,2,128,256]{3,2,1,0:T(8,128)(2,1)S(1)} async-done(((bf16[8,2,128,256]{3,2,1,0:T(8,128)(2,1)}), bf16[8,2,128,256]{3,2,1,0:T(8,128)(2,1)S(1)}, u32[]{:S(2)}, u32[]{:S(2)}) %all-to-all-start.2) | async-done | bytes 1048608 | tf_op jit(solution)/shard_map/all_to_all | solution.py:298
  215.5 1.7 fusion.1
  236.3 4.2 %all-to-all-start.3 = ((bf16[8,2,256,128]{3,2,1,0:T(8,128)(2,1)}), bf16[8,2,256,128]{3,2,1,0:T(8,128)(2,1)}, u32[]{:S(2)}, u32[]{:S(2)}) async-start(bf16[8,2,256,128]{3,2,1,0:T(8,128)(2,1)} %bitcast.104), calls=%async_computation.3 | async-start | bytes 2097152 | tf_op jit(solution)/shard_map/all_to_all | solution.py:298
  242.2 2.9 fusion.12
  245.1 1.9 fusion.29.mix_ref
  247.0 7.5 %right_out.1 = bf16[8,768,128]{2,1,0:T(8,128)(2,1)} custom-call(s32[8]{0:T(128)} %multiply_add_fusion.place_ref, bf16[16,768,128]{2,1,0:T(8,128)(2,1)} %bitcast.96, bf16[8,768,128]{2,1,0:T(8,128)(2,1)} %bitcast.103, bf16[8,256,128]{2,1,0:T(8,128)(2,1)} %fusion.29.mix_ref), custom_call_target="tpu_custom_call" | custom-call | flops 402653184 | bytes 4718592 | tf_op jit(solution)/shard_map/right_out/pallas_call | solution.py:247
  254.5 11.5 %all-to-all-done.3 = bf16[8,2,256,128]{3,2,1,0:T(8,128)(2,1)} async-done(((bf16[8,2,256,128]{3,2,1,0:T(8,128)(2,1)}), bf16[8,2,256,128]{3,2,1,0:T(8,128)(2,1)}, u32[]{:S(2)}, u32[]{:S(2)}) %all-to-all-start.3) | async-done | bytes 1048608 | tf_op jit(solution)/shard_map/all_to_all | solution.py:298
  266.0 15.7 %owner_left.1 = (bf16[16,768,128]{2,1,0:T(8,128)(2,1)}, f32[2,768]{1,0:T(2,128)}) custom-call(s32[16]{0:T(128)} %select_reduce_fusion.from_ref, s32[16]{0:T(128)} %convert_element_type.48.hit_ref, s32[16]{0:T(128)} %bitcast.112, bf16[16,768,128]{2,1,0:T(8,128)(2,1)} %bitcast.101, bf16[16,768,128]{2,1,0:T(8,128)(2,1)} %bitcast.11.upd_ref, ...), custom_call_target="tpu_custom_call" | custom-call | tf_op jit(solution)/shard_map/owner_left/pallas_call | solution.py:215
  281.7 11.8 %scale_rows.1 = f32[2,768]{1,0:T(2,128)} custom-call(f32[2,768]{1,0:T(2,128)} %get-tuple-element.6.x_ref), custom_call_target="tpu_custom_call" | custom-call | tf_op jit(solution)/shard_map/scale_rows/pallas_call | solution.py:139
  (103 shorter events, 39.0 us)
Async XLA Ops:
  0.6 12.9 %copy-start = (bf16[1,16,768,128]{3,2,1,0:T(8,128)(2,1)S(1)}, bf16[1,16,768,128]{3,2,1,0:T(8,128)(2,1)}, u32[]{:S(2)}) copy-start(bf16[1,16,768,128]{3,2,1,0:T(8,128)(2,1)} %param.9) | copy-start | bytes 9437188
  13.6 2.6 copy-start.15
  16.2 5.6 %copy-start.17 = (s32[1,8]{1,0:T(1,128)S(1)}, s32[1,8]{1,0:T(1,128)}, u32[]{:S(2)}) copy-start(s32[1,8]{1,0:T(1,128)} %param.15) | copy-start | bytes 100
  16.2 75.1 %all-to-all-start.1 = ((bf16[8,2,768,128]{3,2,1,0:T(8,128)(2,1)}), bf16[8,2,768,128]{3,2,1,0:T(8,128)(2,1)S(1)}, u32[]{:S(2)}, u32[]{:S(2)}) async-start(bf16[8,2,768,128]{3,2,1,0:T(8,128)(2,1)} %bitcast.99), calls=%async_computation.1 | async-start | bytes 6291456 | tf_op jit(solution)/shard_map/all_to_all | solution.py:298
  91.3 1.7 copy-start.2
  91.3 6.1 %copy-start.14 = (s32[8,1,128]{2,1,0:T(1,128)S(1)}, s32[8,1,128]{2,1,0:T(1,128)}, u32[]{:S(2)}) copy-start(s32[8,1,128]{2,1,0:T(1,128)} %gather_small.1) | copy-start | bytes 12292
  91.3 7.4 %copy-start.18 = (s32[1,8]{1,0:T(1,128)S(1)}, s32[1,8]{1,0:T(1,128)}, u32[]{:S(2)}) copy-start(s32[1,8]{1,0:T(1,128)} %param.14) | copy-start | bytes 100
  93.0 74.6 %all-to-all-start = ((bf16[8,2,768,128]{3,2,1,0:T(8,128)(2,1)}), bf16[8,2,768,128]{3,2,1,0:T(8,128)(2,1)}, u32[]{:S(2)}, u32[]{:S(2)}) async-start(bf16[8,2,768,128]{3,2,1,0:T(8,128)(2,1)} %bitcast.98), calls=%async_computation | async-start | bytes 6291456 | tf_op jit(solution)/shard_map/all_to_all | solution.py:298
  98.0 12.2 %copy-start.12 = (f32[256,256]{1,0:T(8,128)}, f32[256,256]{1,0:T(8,128)S(1)}, u32[]{:S(2)}) copy-start(f32[256,256]{1,0:T(8,128)S(1)} %fusion.53) | copy-start | bytes 786436
  180.4 3.9 %copy-start.8 = (f32[8,256,256]{2,1,0:T(8,128)S(1)}, f32[8,256,256]{2,1,0:T(8,128)}, u32[]{:S(2)}) copy-start(f32[8,256,256]{2,1,0:T(8,128)} %right_gram.1) | copy-start | bytes 6291460
  180.4 30.0 %all-to-all-start.2 = ((bf16[8,2,128,256]{3,2,1,0:T(8,128)(2,1)}), bf16[8,2,128,256]{3,2,1,0:T(8,128)(2,1)S(1)}, u32[]{:S(2)}, u32[]{:S(2)}) async-start(bf16[8,2,128,256]{3,2,1,0:T(8,128)(2,1)} %bitcast.105), calls=%async_computation.2 | async-start | bytes 2097152 | tf_op jit(solution)/shard_map/all_to_all | solution.py:298
  184.3 3.1 %copy-start.13 = (f32[256,256]{1,0:T(8,128)S(1)}, f32[256,256]{1,0:T(8,128)}, u32[]{:S(2)}) copy-start(f32[256,256]{1,0:T(8,128)} %copy-done.12) | copy-start | bytes 786436
  189.3 1.6 copy-start.9
  192.5 1.3 copy-start.7
  193.9 1.3 copy-start.3
  213.1 1.3 copy-start.11
  214.3 1.2 copy-start.10
  232.5 1.0 copy-start.5
  234.6 6.3 %copy-start.16 = (s32[16]{0:T(128)S(1)}, s32[16]{0:T(128)}, u32[]{:S(2)}) copy-start(s32[16]{0:T(128)} %copy-done.15) | copy-start | bytes 196
  234.6 7.6 %copy-start.4 = (f32[8,256,256]{2,1,0:T(8,128)S(1)}, f32[8,256,256]{2,1,0:T(8,128)}, u32[]{:S(2)}) copy-start(f32[8,256,256]{2,1,0:T(8,128)} %copy-done.3) | copy-start | bytes 6291460
  236.3 29.8 %all-to-all-start.3 = ((bf16[8,2,256,128]{3,2,1,0:T(8,128)(2,1)}), bf16[8,2,256,128]{3,2,1,0:T(8,128)(2,1)}, u32[]{:S(2)}, u32[]{:S(2)}) async-start(bf16[8,2,256,128]{3,2,1,0:T(8,128)(2,1)} %bitcast.104), calls=%async_computation.3 | async-start | bytes 2097152 | tf_op jit(solution)/shard_map/all_to_all | solution.py:298
  242.2 2.9 copy-start.6
  266.0 28.8 %copy-start.1 = (bf16[1,16,768,128]{3,2,1,0:T(8,128)(2,1)S(1)}, bf16[1,16,768,128]{3,2,1,0:T(8,128)(2,1)}, u32[]{:S(2)}) copy-start(bf16[1,16,768,128]{3,2,1,0:T(8,128)(2,1)} %param.9) | copy-start | bytes 9437188

commit v2 on v1

--- a/solution.py
+++ b/solution.py
@@ -14,11 +14,6 @@
 ROOTS = 3
 F32 = jnp.float32
 BF16 = jnp.bfloat16
-HIGH = lax.Precision.HIGH
-
-
-def bmm(a, b):
-    return jnp.einsum("bij,bjk->bik", a, b, precision=HIGH, preferred_element_type=F32)
 
 
 def contract_rows(a, b):
@@ -153,28 +148,280 @@
     )(x)
 
 
-def owner_gram_kernel(tile_ref, cur_ref, upd_ref, o_ref):
-    half = cur_ref.shape[1]
-    o_ref[:, :half] = contract_rows(cur_ref[...], cur_ref[...]).astype(BF16)
-    o_ref[:, half:] = contract_rows(cur_ref[...], upd_ref[...]).astype(BF16)
-
-
-def owner_gram(asked, current, arrived):
-    slots, order, half = arrived.shape
+def split(a):
+    upper = a.astype(BF16)
+    return upper, (a - upper.astype(F32)).astype(BF16)
+
+
+def product(a, b, dims=(((1,), (0,)), ((), ()))):
+    dot = functools.partial(lax.dot_general, dimension_numbers=dims, preferred_element_type=F32)
+    return dot(a[0], b[0]) + (dot(a[0], b[1]) + dot(a[1], b[0]))
+
+
+def iota(shape, axis):
+    return lax.broadcasted_iota(jnp.int32, shape, axis)
+
+
+def total(a):
+    return jnp.sum(jnp.sum(a, axis=1, keepdims=True), axis=0, keepdims=True)
+
+
+def sweep_kernel(
+    n,
+    pairs,
+    tab,
+    send_left,
+    send_right,
+    own_left_hbm,
+    add_left_hbm,
+    add_right_hbm,
+    got_left,
+    got_mix,
+    out_right,
+    own_left,
+    add_left,
+    add_right,
+    right_0,
+    right_1,
+    gram_send,
+    gram_0,
+    gram_1,
+    roots,
+    inverses,
+    mixes,
+    mix_send,
+    sends,
+    recvs,
+    locals_,
+):
+    row, me = lax.axis_index("row"), lax.axis_index("col")
+    order, half = got_left.shape[2:]
+    wide = 2 * half
+    slots = CAP * pairs
+    at_tile, at_owner, at_index = 0, CAP * n, CAP * n + slots
+    at_rank, at_add, at_keep = (CAP * n + i * slots for i in (2, 3, 4))
+    at_pack = CAP * n + 5 * slots
+    got_right = (right_0, right_1)
+    got_gram = (gram_0, gram_1)
+
+    loads = []
+    for i, (src, dst) in enumerate(
+        ((own_left_hbm, own_left), (add_left_hbm, add_left), (add_right_hbm, add_right))
+    ):
+        load = pltpu.make_async_copy(src, dst, locals_.at[8, i])
+        load.start()
+        loads.append(load)
+
+    barrier = pltpu.get_barrier_semaphore()
+    for step in range(1, n):
+        pl.semaphore_signal(
+            barrier,
+            inc=1,
+            device_id=(row, lax.rem(me + step, n)),
+            device_id_type=pl.DeviceIdType.MESH,
+        )
+    pl.semaphore_wait(barrier, n - 1)
+
+    def exchange(kind, src, dst):
+        copies = []
+        for step in [s for g in range(1, n // 2 + 1) for s in sorted({g, n - g})]:
+            peer = lax.rem(me + step, n)
+            copy = pltpu.make_async_remote_copy(
+                src_ref=src(peer),
+                dst_ref=dst(me),
+                send_sem=sends.at[kind, step],
+                recv_sem=recvs.at[kind, step],
+                device_id=(row, peer),
+                device_id_type=pl.DeviceIdType.MESH,
+            )
+            copy.start()
+            copies.append(copy)
+        own = pltpu.make_async_copy(src(me), dst(me), locals_.at[kind, 0])
+        own.start()
+        return own, copies
+
+    def arrive(moved):
+        moved[0].wait()
+        for copy in moved[1]:
+            copy.wait_recv()
+
+    def sent(moved):
+        for copy in moved[1]:
+            copy.wait_send()
+
+    def left_of(c):
+        return exchange(c, lambda p: send_left.at[c, p], lambda p: got_left.at[c, p])
+
+    def right_of(c):
+        return exchange(2 + c, lambda p: send_right.at[c, p], lambda p: got_right[c].at[p])
+
+    def gram_of(c):
+        return exchange(4 + c, lambda p: gram_send.at[c, p], lambda p: got_gram[c].at[p])
+
+    def mix_of(c):
+        return exchange(6 + c, lambda p: mix_send.at[c, p], lambda p: got_mix.at[c, p])
+
+    def masks(at):
+        cur, add = tab[at_rank + at], tab[at_add + at]
+        keeps = []
+        for axis in (0, 1):
+            i = iota((wide, wide), axis)
+            keeps.append(((i < half) & (i < cur)) | ((i >= half) & (i - half < add)))
+        return keeps[0] & keeps[1], keeps[0]
+
+    def owner_grams(c):
+        def one(d, _):
+            cur = own_left[tab[at_tile + c * n + d]]
+            both = jnp.concatenate([cur, got_left[c, d]], axis=1)
+            gram_send[c, d] = contract_rows(cur, both).astype(BF16)
+            return 0
+
+        lax.fori_loop(0, n, one, 0)
+
+    def right_stack(c, k):
+        at = c * pairs + k
+        return jnp.concatenate(
+            [got_right[c][tab[at_owner + at]], add_right[tab[at_index + at]]], axis=1
+        )
+
+    def tile_roots(c, k):
+        at = c * pairs + k
+        stack = right_stack(c, k)
+        keep, keep_row = masks(at)
+        diagonal = iota((wide, wide), 0) == iota((wide, wide), 1)
+        identity = jnp.where(diagonal, 1.0, 0.0).astype(F32)
+        gram = jnp.where(keep, contract_rows(stack, stack), 0.0)
+        gram = gram + jnp.where(diagonal & ~keep_row, 1.0, 0.0)
+        scale = jnp.sqrt(total(gram * gram))
+        root = gram * (1.0 / scale)
+        inverse = 1.5 * identity - 0.5 * root
+        root = product(split(root), split(inverse))
+        for _ in range(ROOTS - 1):
+            q, p = split(inverse), split(root)
+            middle = split(1.5 * identity - 0.5 * product(q, p))
+            root = product(p, middle)
+            inverse = product(middle, q)
+        roots[at] = root * jnp.sqrt(scale)
+        inverses[at] = inverse * lax.rsqrt(scale)
+
+    def tile_core(c, k):
+        at = c * pairs + k
+        top = got_gram[c][tab[at_owner + at]].astype(F32)
+        add = add_left[tab[at_index + at]]
+        low = jnp.concatenate([top[:, half:].T, contract_rows(add, add)], axis=1)
+        gram = jnp.concatenate([top, low], axis=0)
+        gram = jnp.where(masks(at)[0], gram, 0.0)
+        root = roots[at]
+        s = split(root)
+        folded = root[:, :half] + root[:, half:]
+        core = product(s, split(product(split(gram), split(folded))))
+        y = core * lax.rsqrt(total(core * core) + 1e-06)
+        for _ in range(SWEEPS):
+            ys = split(y)
+            inner = product(ys, ys, (((0,), (0,)), ((), ())))
+            y = 1.5 * y - 0.5 * product(ys, split(inner))
+        y = split(jnp.where(iota(y.shape, 1) < tab[at_keep + at], y, 0.0))
+        mixes[at] = product(s, y).astype(BF16)
+        mix = product(split(inverses[at]), y) * math.sqrt(order)
+        return mix.astype(BF16)
+
+    def each(c, work, many):
+        def some(i, _):
+            for j in range(many):
+                work(c, i * many + j)
+            return 0
+
+        lax.fori_loop(0, pairs // many, some, 0)
+
+    many = 2 if pairs % 2 == 0 else 1
+    mixes_right = inverses
+
+    def finish_core(c, k):
+        mixes_right[c * pairs + k, :, :half] = tile_core(c, k).astype(F32)
+
+    def right_out(c, k):
+        at = c * pairs + k
+        mix = mixes_right[at, :, :half].astype(BF16)
+        out_right[at] = jnp.dot(
+            right_stack(c, k), mix, preferred_element_type=F32
+        ).astype(BF16)
+
+    def pack(c):
+        def one(o, _):
+            mix_send[c, o] = mixes[tab[at_pack + c * n + o]]
+            return 0
+
+        lax.fori_loop(0, n, one, 0)
+
+    left_a = left_of(0)
+    right_a = right_of(0)
+    left_b = left_of(1)
+    for load in loads:
+        load.wait()
+    arrive(left_a)
+    owner_grams(0)
+    gram_a = gram_of(0)
+    right_b = right_of(1)
+    arrive(right_a)
+    each(0, tile_roots, many)
+    arrive(left_b)
+    owner_grams(1)
+    gram_b = gram_of(1)
+    arrive(gram_a)
+    each(0, finish_core, many)
+    pack(0)
+    mix_a = mix_of(0)
+    each(0, right_out, many)
+    arrive(right_b)
+    each(1, tile_roots, many)
+    arrive(gram_b)
+    each(1, finish_core, many)
+    pack(1)
+    mix_b = mix_of(1)
+    each(1, right_out, many)
+    arrive(mix_a)
+    arrive(mix_b)
+    for moved in (left_a, right_a, left_b, gram_a, right_b, gram_b, mix_a, mix_b):
+        sent(moved)
+
+
+def sweep(tab, send_left, send_right, own_left, add_left, add_right, n):
+    tiles, order, half = own_left.shape
+    slots = add_left.shape[0]
+    wide = 2 * half
+    vmem = pl.BlockSpec(memory_space=pltpu.VMEM)
+    hbm = pl.BlockSpec(memory_space=pl.ANY)
     return pl.pallas_call(
-        owner_gram_kernel,
-        grid_spec=pltpu.PrefetchScalarGridSpec(
-            num_scalar_prefetch=1,
-            grid=(slots,),
-            in_specs=[
-                pl.BlockSpec((None, order, half), lambda s, t: (t[s], 0, 0)),
-                pl.BlockSpec((None, order, half), lambda s, t: (s, 0, 0)),
-            ],
-            out_specs=pl.BlockSpec((None, half, 2 * half), lambda s, t: (s, 0, 0)),
+        functools.partial(sweep_kernel, n, slots // CAP),
+        in_specs=[pl.BlockSpec(memory_space=pltpu.SMEM)] + [hbm] * 5,
+        out_specs=[vmem] * 3,
+        out_shape=[
+            jax.ShapeDtypeStruct((CAP, n, order, half), BF16),
+            jax.ShapeDtypeStruct((CAP, n, wide, half), BF16),
+            jax.ShapeDtypeStruct((slots, order, half), BF16),
+        ],
+        scratch_shapes=[
+            pltpu.VMEM((tiles, order, half), BF16),
+            pltpu.VMEM((slots, order, half), BF16),
+            pltpu.VMEM((slots, order, half), BF16),
+            pltpu.VMEM((n, order, half), BF16),
+            pltpu.VMEM((n, order, half), BF16),
+            pltpu.VMEM((CAP, n, half, wide), BF16),
+            pltpu.VMEM((n, half, wide), BF16),
+            pltpu.VMEM((n, half, wide), BF16),
+            pltpu.VMEM((slots, wide, wide), F32),
+            pltpu.VMEM((slots, wide, wide), F32),
+            pltpu.VMEM((slots, wide, half), BF16),
+            pltpu.VMEM((CAP, n, wide, half), BF16),
+            pltpu.SemaphoreType.DMA((8, n)),
+            pltpu.SemaphoreType.DMA((8, n)),
+            pltpu.SemaphoreType.DMA((9, 3)),
+        ],
+        compiler_params=pltpu.CompilerParams(
+            collective_id=2, has_side_effects=True, vmem_limit_bytes=60 * 1024 * 1024
         ),
-        out_shape=jax.ShapeDtypeStruct((slots, half, 2 * half), BF16),
-        name="owner_gram",
-    )(asked, current, arrived)
+        name="sweep",
+    )(tab, send_left, send_right, own_left, add_left, add_right)
 
 
 def owner_left_kernel(from_ref, hit_ref, rank_ref, cur_ref, upd_ref, mix_ref, o_ref, sum_ref):
@@ -235,72 +482,12 @@
     )(arrival, hit, rank, current, arrived, mix)
 
 
-def right_kernel(place_ref, cur_ref, upd_ref, mix_ref, o_ref):
-    half = cur_ref.shape[1]
-    fresh = jnp.dot(cur_ref[...], mix_ref[:half], preferred_element_type=F32)
-    fresh += jnp.dot(upd_ref[...], mix_ref[half:], preferred_element_type=F32)
-    o_ref[...] = fresh.astype(BF16)
-
-
-def right_out(place, received, update, mix):
-    slots, order, half = update.shape
-    return pl.pallas_call(
-        right_kernel,
-        grid_spec=pltpu.PrefetchScalarGridSpec(
-            num_scalar_prefetch=1,
-            grid=(slots,),
-            in_specs=[
-                pl.BlockSpec((None, order, half), lambda j, p: (p[j], 0, 0)),
-                pl.BlockSpec((None, order, half), lambda j, p: (j, 0, 0)),
-                pl.BlockSpec((None, 2 * half, half), lambda j, p: (j, 0, 0)),
-            ],
-            out_specs=pl.BlockSpec((None, order, half), lambda j, p: (j, 0, 0)),
-        ),
-        out_shape=jax.ShapeDtypeStruct((slots, order, half), BF16),
-        cost_estimate=pl.CostEstimate(
-            flops=4 * slots * order * half * half,
-            bytes_accessed=6 * slots * order * half,
-            transcendentals=0,
-        ),
-        name="right_out",
-    )(place, received, update, mix)
-
-
-def right_gram_kernel(place_ref, cur_ref, upd_ref, o_ref):
-    half = cur_ref.shape[1]
-    cross = contract_rows(cur_ref[...], upd_ref[...])
-    o_ref[:half, :half] = contract_rows(cur_ref[...], cur_ref[...])
-    o_ref[:half, half:] = cross
-    o_ref[half:, :half] = cross.T
-    o_ref[half:, half:] = contract_rows(upd_ref[...], upd_ref[...])
-
-
-def right_gram(place, received, update):
-    slots, order, half = update.shape
-    return pl.pallas_call(
-        right_gram_kernel,
-        grid_spec=pltpu.PrefetchScalarGridSpec(
-            num_scalar_prefetch=1,
-            grid=(slots,),
-            in_specs=[
-                pl.BlockSpec((None, order, half), lambda j, p: (p[j], 0, 0)),
-                pl.BlockSpec((None, order, half), lambda j, p: (j, 0, 0)),
-            ],
-            out_specs=pl.BlockSpec((None, 2 * half, 2 * half), lambda j, p: (j, 0, 0)),
-        ),
-        out_shape=jax.ShapeDtypeStruct((slots, 2 * half, 2 * half), F32),
-        name="right_gram",
-    )(place, received, update)
-
-
-def swap(values, n):
-    shaped = values.reshape((n, CAP) + values.shape[1:])
-    out = lax.all_to_all(shaped, "col", split_axis=0, concat_axis=0, tiled=True)
-    return out.reshape(values.shape)
-
-
 def take(values, index):
     return jnp.take(values, index, axis=0, mode="clip")
+
+
+def pick(mask, values):
+    return jnp.sum(jnp.where(mask, values, 0), axis=-1).astype(jnp.int32)
 
 
 def local(
@@ -320,15 +507,21 @@
     add_left, add_right = update_left[0], update_right[0]
     tiles, order, half = own_left.shape
     slots = owner_slot.shape[1]
+    pairs = slots // CAP
     slot_index = jnp.arange(slots)
 
     mine = owner_slot[0]
     owner = mine // tiles
-    earlier = (owner[:, None] == owner[None, :]) & (slot_index[None, :] < slot_index[:, None])
-    place = owner * CAP + jnp.sum(earlier.astype(jnp.int32), axis=1)
-    chosen = place[None, :] == jnp.arange(n * CAP)[:, None]
-    source = jnp.sum(jnp.where(chosen, slot_index[None, :], 0), axis=1)
-    arrived_left = swap(take(add_left, source), n)
+    which = pick(
+        (owner[:, None] == owner[None, :]) & (slot_index[None, :] < slot_index[:, None]), 1
+    )
+    place = which * n + owner
+    chosen = place[None, :] == jnp.arange(CAP * n)[:, None]
+    source = pick(chosen, slot_index[None, :])
+    send_left = take(add_left, source).reshape((CAP, n, order, half))
+    rank_in = pick(place[None, :] < place[:, None], 1)
+    to_slot = pick(rank_in[None, :] == slot_index[:, None], slot_index[None, :])
+    pack = pick(chosen, rank_in[None, :])
 
     packed = jnp.concatenate([mine, current_rank[0], target_rank[0]])
     width = -(-packed.shape[0] // 128) * 128
@@ -337,69 +530,42 @@
     named = table[:, :slots]
     ranks = table[:, slots : slots + tiles].reshape(-1)
     targets = table[:, slots + tiles : slots + 2 * tiles].reshape(-1)
-    my_rank = jnp.sum(
-        jnp.where(mine[:, None] == jnp.arange(n * tiles)[None, :], ranks[None, :], 0), axis=1
-    )
-    my_target = jnp.sum(
-        jnp.where(mine[:, None] == jnp.arange(n * tiles)[None, :], targets[None, :], 0), axis=1
-    )
+    of_mine = mine[:, None] == jnp.arange(n * tiles)[None, :]
+    per_slot = jnp.stack(
+        [
+            owner,
+            slot_index,
+            pick(of_mine, ranks[None, :]),
+            update_rank[0],
+            pick(of_mine, targets[None, :]),
+        ]
+    )
+    in_order = pick((to_slot[:, None] == slot_index[None, :])[None], per_slot[:, None, :])
     to_me = (named // tiles) == me
-    count = jnp.sum(
-        (to_me[:, None, :] & (slot_index[None, None, :] < slot_index[None, :, None])).astype(
-            jnp.int32
-        ),
-        axis=2,
-    )
-    picked = to_me[:, None, :] & (count[:, None, :] == jnp.arange(CAP)[None, :, None])
-    asked = jnp.sum(jnp.where(picked, (named % tiles)[:, None, :], 0), axis=2).reshape(-1)
+    count = pick(
+        to_me[:, None, :] & (slot_index[None, None, :] < slot_index[None, :, None]), 1
+    )
+    picked = to_me[None] & (count[None] == jnp.arange(CAP)[:, None, None])
+    asked = pick(picked, (named % tiles)[None]).reshape(-1)
     asked_used = jnp.any(picked, axis=2).reshape(-1)
-
-    received_right = swap(take(own_right, asked), n)
-    grams = swap(owner_gram(asked, own_left, arrived_left), n)
-
-    column = jnp.arange(2 * half)[None, :]
-    live = jnp.where(
-        column < half, column < my_rank[:, None], column - half < update_rank[0][:, None]
-    ).astype(F32)
-    both = live[:, :, None] * live[:, None, :]
-    identity = jnp.eye(2 * half, dtype=F32)
-    gram_right = right_gram(place, received_right, add_right) * both
-    gram_right = gram_right + identity * (1.0 - live)[:, :, None]
-    c = jnp.sqrt(jnp.sum(gram_right * gram_right, axis=(1, 2), keepdims=True))
-    root = gram_right / c
-    inverse = 1.5 * identity - 0.5 * root
-    root = bmm(root, inverse)
-    for _ in range(ROOTS - 1):
-        middle = 1.5 * identity - 0.5 * bmm(inverse, root)
-        root = bmm(root, middle)
-        inverse = bmm(middle, inverse)
-    root = root * jnp.sqrt(c)
-    inverse = inverse * lax.rsqrt(c)
-
-    own_gram = jnp.einsum("bki,bkj->bij", add_left, add_left, preferred_element_type=F32)
-    top = take(grams, place).astype(F32)
-    low = jnp.concatenate([jnp.swapaxes(top[:, :, half:], 1, 2), own_gram], axis=2)
-    gram_left = jnp.concatenate([top, low], axis=1) * both
-    core = bmm(root, gram_left)
-    core = bmm(core, root[:, :, :half] + root[:, :, half:])
-    y = core * lax.rsqrt(jnp.sum(core * core, axis=(1, 2), keepdims=True) + 1e-06)
-    for _ in range(SWEEPS):
-        inner = jnp.einsum("bki,bkj->bij", y, y, precision=HIGH, preferred_element_type=F32)
-        y = 1.5 * y - 0.5 * bmm(y, inner)
-    y = y * (jnp.arange(half)[None, :] < my_target[:, None]).astype(F32)[:, None, :]
-    mix_left = (bmm(root, y) * live[:, :, None]).astype(BF16)
-    mix_right = (bmm(inverse, y) * (live[:, :, None] * math.sqrt(order))).astype(BF16)
-
-    arrived_mix = swap(take(mix_left, source), n)
-    returned_right = right_out(place, received_right, add_right, mix_right)
+    send_right = take(own_right, asked).reshape((CAP, n, order, half))
+
+    tab = jnp.concatenate([asked, in_order.reshape(-1), pack])
+    arrived_left, arrived_mix, right = sweep(
+        tab, send_left, send_right, own_left, add_left, add_right, n
+    )
+    returned_right = take(right, rank_in)
 
     matched = (asked[None, :] == jnp.arange(tiles)[:, None]) & asked_used[None, :]
     hit = jnp.any(matched, axis=1).astype(jnp.int32)
-    arrival = jnp.sum(
-        jnp.where(matched, jnp.arange(n * CAP)[None, :], 0), axis=1
-    ).astype(jnp.int32)
+    arrival = pick(matched, jnp.arange(n * CAP)[None, :])
     kept, partial = owner_left(
-        arrival, hit, current_rank[0], own_left, arrived_left, arrived_mix
+        arrival,
+        hit,
+        current_rank[0],
+        own_left,
+        arrived_left.reshape((CAP * n, order, half)),
+        arrived_mix.reshape((CAP * n, 2 * half, half)),
     )
     return (kept[None], returned_right[None], scale_rows(partial, n, m))
 

time: 296 us -> 263 us (0.89)
  Pallas kernels: 65.3 us -> 238 us
  waiting for transfers between devices: 146 us -> 0 us
  matrix products: 36.5 us -> 0 us
  starting transfers between devices: 18.1 us -> 0 us
  local copies, waits for them, and re-layouts: 20 us -> 13.7 us
    pallas_call x3 -> x1, Pallas kernels: 28.3 us -> 200 us  [sweep(): pl.pallas_call(functools.partial(sweep_kernel, n, slots // CAP), in_specs...]
    all_to_all x4 -> x0, waiting for transfers between devices: 146 us -> none  [swap(): out = lax.all_to_all(shaped, 'col', split_axis=0, concat_axis=0, tiled=True)]
    dot_general x28 -> x0, matrix products: 36.5 us -> none  [the longest x19 24.7 us: bmm(): jnp.einsum('bij,bjk->bik', a, b, precision=HIGH, preferred_element_type=F32)]
    all_to_all x4 -> x0, starting transfers between devices: 18.1 us -> none  [swap(): out = lax.all_to_all(shaped, 'col', split_axis=0, concat_axis=0, tiled=True)]
    unnamed x39 -> x3, local copies, waits for them, and re-layouts: 6.68 us -> 1.3 us
    pallas_call x1, Pallas kernels: 11.8 us -> 14.8 us  [scale_rows(): pl.pallas_call(functools.partial(scale_kernel, n, m), out_shape=jax.Shape...]
    gather x5 -> x3, local copies, waits for them, and re-layouts: 11 us -> 9.97 us  [take(): return jnp.take(values, index, axis=0, mode='clip')]
  transfers between devices with their start and end apart: 4 -> 0, of which waited for: 4 -> 0; matrix products, arithmetic and copies ran while one was open for 10% -> 0% of each run, Pallas kernels for 5% -> 0%
where the time goes in v2:
time: 263 us; the launch traced here: 262 us
  Pallas kernels  238 us (90%)
  local copies, waits for them, and re-layouts  13.7 us (5%)
  other arithmetic  9.74 us (4%)
    pallas_call x1, Pallas kernels, sweep(): pl.pallas_call(functools.partial(sweep_kernel, n, slots // CAP), in_specs...  200 us
    pallas_call x1, Pallas kernels, scale_rows(): pl.pallas_call(functools.partial(scale_kernel, n, m), out_shape=jax.Shape...  14.8 us
    pallas_call x1, Pallas kernels, owner_left(): pl.pallas_call(owner_left_kernel, grid_spec=pltpu.PrefetchScalarGridSpec(...  13.5 us
    gather x3, local copies, waits for them, and re-layouts, take(): return jnp.take(values, index, axis=0, mode='clip')  9.97 us
    pallas_call x1, Pallas kernels, gather_small(): pl.pallas_call(functools.partial(gather_kernel, n), out_shape=jax.ShapeDt...  9.55 us

profile of v2, /device:TPU:0, one launch (start us, length us, event | category | flops | bytes accessed | tf_op | source)
XLA Modules:
  0.0 262.1 jit_solution(2911714121824526136)
XLA Ops:
  0.6 0.9 pad_add_fusion
  1.6 0.5 pad_bitcast_fusion.x_ref
  2.1 9.5 %gather_small.1 = s32[8,1,128]{2,1,0:T(1,128)} custom-call(s32[1,128]{1,0:T(1,128)} %pad_bitcast_fusion.x_ref), custom_call_target="tpu_custom_call" | custom-call | tf_op jit(solution)/shard_map/gather_small/pallas_call | solution.py:53
  11.6 0.7 fusion.4
  12.3 0.7 add_select_fusion
  13.0 0.2 select_reduce_fusion
  13.7 0.6 select_reduce_fusion.2.from_ref
  14.5 0.5 convert_element_type.3.hit_ref
  15.0 0.7 fusion.9
  15.7 0.7 and_select_fusion.1
  16.5 0.7 fusion.7
  17.2 0.7 multiply_add_fusion
  18.1 0.7 and_select_fusion
  18.8 0.8 fusion.8
  19.8 0.9 select_reduce_fusion.6
  20.7 0.7 stack.13
  21.8 0.6 pad_add_fusion.1.tab
  22.4 4.0 %gather_fusion = bf16[16,768,128]{2,1,0:T(8,128)(2,1)} fusion(bf16[8,768,128]{2,1,0:T(8,128)(2,1)} %bitcast.30, s32[1024]{0:T(1024)S(1)} %pad_clamp_fusion.2), kind=kCustom, calls=%fused_computation | custom fusion | bytes 6291520 | tf_op jit(solution)/shard_map/jit(_take)/gather | solution.py:486
  26.4 2.7 %gather_fusion.1 = bf16[16,768,128]{2,1,0:T(8,128)(2,1)} fusion(bf16[16,768,128]{2,1,0:T(8,128)(2,1)S(1)} %bitcast.29, s32[1024]{0:T(1024)S(1)} %pad_clamp_fusion.1), kind=kCustom, calls=%fused_computation.1 | custom fusion | bytes 6291520 | tf_op jit(solution)/shard_map/jit(_take)/gather | solution.py:486
  29.1 200.2 %sweep.1 = (bf16[2,8,768,128]{3,2,1,0:T(8,128)(2,1)}, bf16[2,8,256,128]{3,2,1,0:T(8,128)(2,1)}, bf16[8,768,128]{2,1,0:T(8,128)(2,1)}) custom-call(s32[72]{0:T(128)} %pad_add_fusion.1.tab, bf16[2,8,768,128]{3,2,1,0:T(8,128)(2,1)} %bitcast.32, bf16[2,8,768,128]{3,2,1,0:T(8,128)(2,1)} %bitcast.33, bf16[16,768,128]{2,1,0:T(8,128)(2,1)} %bitcast.34, ...), custom_call_target="tpu_custom_call" | custom-call | tf_op jit(solution)/shard_map/sweep/pallas_call | solution.py:394
  229.3 13.5 %owner_left.1 = (bf16[16,768,128]{2,1,0:T(8,128)(2,1)}, f32[2,768]{1,0:T(2,128)}) custom-call(s32[16]{0:T(128)} %select_reduce_fusion.2.from_ref, s32[16]{0:T(128)} %convert_element_type.3.hit_ref, s32[16]{0:T(128)} %bitcast.44, bf16[16,768,128]{2,1,0:T(8,128)(2,1)} %bitcast.35, bf16[16,768,128]{2,1,0:T(8,128)(2,1)} %bitcast.36, bf16[16,256,128]{2,1,0:T(8,128)(2,1)} %bitcast.39), custom_call_target="tpu_custom_call" | custom-call | tf_op jit(solution)/shard_map/owner_left/pallas_call | solution.py:462
  242.8 3.3 %gather_fusion.2 = bf16[8,768,128]{2,1,0:T(8,128)(2,1)} fusion(bf16[8,768,128]{2,1,0:T(8,128)(2,1)} %get-tuple-element.11, s32[1024]{0:T(1024)S(1)} %pad_clamp_fusion), kind=kCustom, calls=%fused_computation.2 | custom fusion | bytes 3145760 | tf_op jit(solution)/shard_map/jit(_take)/gather | solution.py:486
  246.1 14.8 %scale_rows.1 = f32[2,768]{1,0:T(2,128)} custom-call(f32[2,768]{1,0:T(2,128)} %get-tuple-element.12.x_ref), custom_call_target="tpu_custom_call" | custom-call | tf_op jit(solution)/shard_map/scale_rows/pallas_call | solution.py:134
  260.9 1.3 copy.12
  (20 shorter events, 1.7 us)
Async XLA Ops:
  0.6 25.8 %copy-start = (bf16[1,16,768,128]{3,2,1,0:T(8,128)(2,1)S(1)}, bf16[1,16,768,128]{3,2,1,0:T(8,128)(2,1)}, u32[]{:S(2)}) copy-start(bf16[1,16,768,128]{3,2,1,0:T(8,128)(2,1)} %param.9) | copy-start | bytes 9437188

commit v3 on v2

v3 whole, which is shorter than its diff:
```python
import functools
import math

import jax
import jax.numpy as jnp
from jax import lax
from jax.experimental import pallas as pl
from jax.experimental.pallas import tpu as pltpu
from jax.sharding import PartitionSpec as P

CAP = 2
BR = 2
SWEEPS = 8
ROOTS = 3
F32 = jnp.float32
BF16 = jnp.bfloat16


def contract_rows(a, b):
    return lax.dot_general(a, b, (((0,), (0,)), ((), ())), preferred_element_type=F32)


def split(a):
    upper = a.astype(BF16)
    return upper, (a - upper.astype(F32)).astype(BF16)


def product(a, b, dims=(((1,), (0,)), ((), ()))):
    dot = functools.partial(lax.dot_general, dimension_numbers=dims, preferred_element_type=F32)
    return dot(a[0], b[0]) + (dot(a[0], b[1]) + dot(a[1], b[0]))


def iota(shape, axis):
    return lax.broadcasted_iota(jnp.int32, shape, axis)


def total(a):
    return jnp.sum(jnp.sum(a, axis=1, keepdims=True), axis=0, keepdims=True)


def sweep_kernel(
    n,
    m,
    mine,
    packed,
    own_left_hbm,
    own_right_hbm,
    add_left_hbm,
    add_right_hbm,
    kept_left,
    out_right,
    out_scale,
    own_left,
    own_right,
    add_left,
    add_right,
    send_left,
    send_right,
    got_left,
    right_0,
    right_1,
    gram_send,
    gram_0,
    gram_1,
    roots,
    inverses,
    mixes,
    mix_send,
    got_mix,
    made_right,
    squares,
    rows,
    parts,
    mine_total,
    totals,
    table_vmem,
    table,
    tab,
    sends,
    recvs,
    row_sems,
    locals_,
):
    row, me = lax.axis_index("row"), lax.axis_index("col")
    order, half = got_left.shape[2:]
    wide = 2 * half
    tiles, slots = own_left.shape[0], add_left.shape[0]
    pairs = slots // CAP
    at_tile, at_source, at_used, at_seq, at_has = 0, CAP * n, 2 * CAP * n, 3 * CAP * n, 4 * CAP * n
    at_owner, at_index, at_rank, at_add, at_keep = (5 * CAP * n + i * slots for i in range(5))
    at_arrival = 5 * CAP * n + 5 * slots
    at_hit = at_arrival + tiles
    got_right = (right_0, right_1)
    got_gram = (gram_0, gram_1)

    loads = []
    for i, (src, dst) in enumerate(
        (
            (add_left_hbm, add_left),
            (own_right_hbm, own_right),
            (own_left_hbm, own_left),
            (add_right_hbm, add_right),
        )
    ):
        load = pltpu.make_async_copy(src, dst, locals_.at[9, i])
        load.start()
        loads.append(load)

    barrier = pltpu.get_barrier_semaphore()
    for step in range(1, n):
        pl.semaphore_signal(
            barrier,
            inc=1,
            device_id=(row, lax.rem(me + step, n)),
            device_id_type=pl.DeviceIdType.MESH,
        )
    for step in range(1, m):
        pl.semaphore_signal(
            barrier,
            inc=1,
            device_id=(lax.rem(row + step, m), me),
            device_id_type=pl.DeviceIdType.MESH,
        )

    def slots_of(owner, held):
        count, found = jnp.int32(0), [jnp.int32(0)] * CAP
        for j in range(slots):
            hit = lax.div(held(j), tiles) == owner
            for c in range(CAP):
                found[c] = jnp.where(hit & (count == c), j, found[c])
            count = count + jnp.where(hit, 1, 0)
        return jnp.where(count > 0, 1, 0), found

    def my_owner(o, before):
        has, found = slots_of(o, lambda j: mine[0, j])
        for c in range(CAP):
            tab[at_source + c * n + o] = found[c]
        tab[at_seq + o] = jnp.minimum(before, pairs - 1)
        tab[at_has + o] = has
        return before + has

    lax.fori_loop(0, n, my_owner, jnp.int32(0))

    def pack_left(c):
        def one(o, _):
            send_left[c, o] = add_left[tab[at_source + c * n + o]]
            return 0

        lax.fori_loop(0, n, one, 0)

    loads[0].wait()
    pack_left(0)
    pack_left(1)
    pl.semaphore_wait(barrier, n + m - 2)

    def exchange(kind, src, dst):
        copies = []
        for step in [s for g in range(1, n // 2 + 1) for s in sorted({g, n - g})]:
            peer = lax.rem(me + step, n)
            copy = pltpu.make_async_remote_copy(
                src_ref=src(peer),
                dst_ref=dst(me),
                send_sem=sends.at[kind, step],
                recv_sem=recvs.at[kind, step],
                device_id=(row, peer),
                device_id_type=pl.DeviceIdType.MESH,
            )
            copy.start()
            copies.append(copy)
        own = pltpu.make_async_copy(src(me), dst(me), locals_.at[kind, 0])
        own.start()
        return own, copies

    def arrive(moved):
        moved[0].wait()
        for copy in moved[1]:
            copy.wait_recv()

    def sent(moved):
        for copy in moved[1]:
            copy.wait_send()

    def row_of(p):
        return table_vmem.at[p]

    def left_of(c):
        return exchange(c, lambda p: send_left.at[c, p], lambda p: got_left.at[c, p])

    def right_of(c):
        return exchange(2 + c, lambda p: send_right.at[c, p], lambda p: got_right[c].at[p])

    def gram_of(c):
        return exchange(4 + c, lambda p: gram_send.at[c, p], lambda p: got_gram[c].at[p])

    def mix_of(c):
        return exchange(6 + c, lambda p: mix_send.at[c, p], lambda p: got_mix.at[c, p])

    def masks(at):
        cur, add = tab[at_rank + at], tab[at_add + at]
        keeps = []
        for axis in (0, 1):
            i = iota((wide, wide), axis)
            keeps.append(((i < half) & (i < cur)) | ((i >= half) & (i - half < add)))
        return keeps[0] & keeps[1], keeps[0]

    def owner_grams(c):
        def one(d, _):
            cur = own_left[tab[at_tile + c * n + d]]
            both = jnp.concatenate([cur, got_left[c, d]], axis=1)
            gram_send[c, d] = contract_rows(cur, both).astype(BF16)
            return 0

        lax.fori_loop(0, n, one, 0)

    def right_stack(c, k):
        at = c * pairs + k
        return jnp.concatenate(
            [got_right[c][tab[at_owner + at]], add_right[tab[at_index + at]]], axis=1
        )

    def tile_roots(c, k):
        at = c * pairs + k
        stack = right_stack(c, k)
        keep, keep_row = masks(at)
        diagonal = iota((wide, wide), 0) == iota((wide, wide), 1)
        identity = jnp.where(diagonal, 1.0, 0.0).astype(F32)
        gram = jnp.where(keep, contract_rows(stack, stack), 0.0)
        gram = gram + jnp.where(diagonal & ~keep_row, 1.0, 0.0)
        scale = jnp.sqrt(total(gram * gram))
        root = gram * (1.0 / scale)
        inverse = 1.5 * identity - 0.5 * root
        root = product(split(root), split(inverse))
        for _ in range(ROOTS - 1):
            q, p = split(inverse), split(root)
            middle = split(1.5 * identity - 0.5 * product(q, p))
            root = product(p, middle)
            inverse = product(middle, q)
        roots[at] = root * jnp.sqrt(scale)
        inverses[at] = inverse * lax.rsqrt(scale)

    def tile_core(c, k):
        at = c * pairs + k
        top = got_gram[c][tab[at_owner + at]].astype(F32)
        add = add_left[tab[at_index + at]]
        low = jnp.concatenate([top[:, half:].T, contract_rows(add, add)], axis=1)
        gram = jnp.concatenate([top, low], axis=0)
        gram = jnp.where(masks(at)[0], gram, 0.0)
        root = roots[at]
        s = split(root)
        folded = root[:, :half] + root[:, half:]
        core = product(s, split(product(split(gram), split(folded))))
        y = core * lax.rsqrt(total(core * core) + 1e-06)
        for _ in range(SWEEPS):
            ys = split(y)
            inner = product(ys, ys, (((0,), (0,)), ((), ())))
            y = 1.5 * y - 0.5 * product(ys, split(inner))
        y = split(jnp.where(iota(y.shape, 1) < tab[at_keep + at], y, 0.0))
        mixes[at] = product(s, y).astype(BF16)
        mix = product(split(inverses[at]), y) * math.sqrt(order)
        return mix.astype(BF16)

    def each(c, work, many):
        def some(i, _):
            for j in range(many):
                work(c, i * many + j)
            return 0

        lax.fori_loop(0, pairs // many, some, 0)

    many = 2 if pairs % 2 == 0 else 1
    mixes_right = inverses

    def finish_core(c, k):
        mixes_right[c * pairs + k, :, :half] = tile_core(c, k).astype(F32)

    def right_out(c, k):
        at = c * pairs + k
        mix = mixes_right[at, :, :half].astype(BF16)
        made_right[at] = jnp.dot(
            right_stack(c, k), mix, preferred_element_type=F32
        ).astype(BF16)

    def pack(c):
        def one(o, _):
            mix_send[c, o] = mixes[c * pairs + tab[at_seq + o]]
            return 0

        lax.fori_loop(0, n, one, 0)

    def index_tables():
        for k in range(pairs):

            def one(o, found):
                chosen = (tab[at_has + o] > 0) & (tab[at_seq + o] == k)
                new = [o] + [tab[at_source + c * n + o] for c in range(CAP)]
                return tuple(jnp.where(chosen, a, b) for a, b in zip(new, found))

            found = lax.fori_loop(0, n, one, (jnp.int32(0),) * (CAP + 1))
            for c in range(CAP):
                at, j = c * pairs + k, found[1 + c]
                tile = lax.rem(mine[0, j], tiles)
                tab[at_owner + at] = found[0]
                tab[at_index + at] = j
                tab[at_rank + at] = table[found[0], 0, slots + tile]
                tab[at_keep + at] = table[found[0], 0, slots + tiles + tile]
                tab[at_add + at] = mine[0, slots + 2 * tiles + j]

    def asked_tables():
        def one(d, _):
            has, found = slots_of(me, lambda j: table[d, 0, j])
            for c in range(CAP):
                tab[at_tile + c * n + d] = lax.rem(table[d, 0, found[c]], tiles)
                tab[at_used + c * n + d] = has
            return 0

        lax.fori_loop(0, n, one, 0)

    def arrival_tables():
        def tile(t, _):
            def one(s, found):
                hit = (tab[at_tile + s] == t) & (tab[at_used + s] > 0)
                return jnp.where(hit, s, found[0]), jnp.where(hit, 1, found[1])

            found = lax.fori_loop(0, CAP * n, one, (jnp.int32(0), jnp.int32(0)))
            tab[at_arrival + t] = found[0]
            tab[at_hit + t] = found[1]
            return 0

        lax.fori_loop(0, tiles, tile, 0)

    def pack_right():
        def one(d, _):
            for c in range(CAP):
                send_right[c, d] = own_right[tab[at_tile + c * n + d]]
            return 0

        lax.fori_loop(0, n, one, 0)

    fresh = send_right

    def new_left(c):
        def one(d, _):
            both = jnp.concatenate([own_left[tab[at_tile + c * n + d]], got_left[c, d]], axis=1)
            made = jnp.dot(both, got_mix[c, d], preferred_element_type=F32)
            fresh[c, d] = made.astype(BF16)
            return 0

        lax.fori_loop(0, n, one, 0)

    def keep_tiles():
        squares[...] = jnp.zeros_like(squares)

        def one(i, _):
            for b in range(BR):
                t = i * BR + b
                s = tab[at_arrival + t]
                hit = tab[at_hit + t] > 0
                limit = jnp.where(hit, 0, mine[0, slots + t])
                column = iota((order, half), 1)
                old = jnp.where(column < limit, own_left[t].astype(F32), 0.0)
                new = fresh[lax.div(s, n), lax.rem(s, n)].astype(F32)
                kept = jnp.where(hit, new, old)
                kept_left[t] = kept.astype(BF16)
                squares[b] += kept * kept
            return 0

        lax.fori_loop(0, tiles // BR, one, 0)
        for b in range(BR):
            sums = lax.dot_general(
                jnp.ones((8, half), F32),
                squares[b],
                (((1,), (1,)), ((), ())),
                precision=lax.Precision.HIGHEST,
                preferred_element_type=F32,
            )
            rows[0, b : b + 1] = sums[:1]

    def local_copy(src, dst, i):
        copy = pltpu.make_async_copy(src, dst, locals_.at[10, i])
        copy.start()
        copy.wait()

    def scale_rows():
        local_copy(rows.at[0], rows.at[1], 0)
        moved = exchange(9, lambda p: rows.at[1], lambda p: parts.at[p])
        arrive(moved)
        row_sum = jnp.sum(parts[...], axis=0)
        mine_total[0] = jnp.broadcast_to(total(row_sum), mine_total.shape[1:])
        local_copy(mine_total.at[0], mine_total.at[1], 1)
        copies = []
        for step in range(1, m):
            copy = pltpu.make_async_remote_copy(
                src_ref=mine_total.at[1],
                dst_ref=totals.at[row],
                send_sem=row_sems.at[0, step],
                recv_sem=row_sems.at[1, step],
                device_id=(lax.rem(row + step, m), me),
                device_id_type=pl.DeviceIdType.MESH,
            )
            copy.start()
            copies.append(copy)
        local_copy(mine_total.at[1], totals.at[row], 2)
        for copy in copies:
            copy.wait()
        everything = jnp.sum(totals[...], axis=0)[:1, :1]
        out_scale[...] = jnp.sqrt(row_sum / (everything * (1.0 / (m * BR * order))))
        sent(moved)

    routes = exchange(8, lambda p: packed, row_of)
    left_a = left_of(0)
    arrive(routes)
    local_copy(table_vmem, table, 3)
    asked_tables()
    loads[1].wait()
    pack_right()
    right_a = right_of(0)
    left_b = left_of(1)
    index_tables()
    arrival_tables()
    loads[2].wait()
    loads[3].wait()
    arrive(left_a)
    owner_grams(0)
    gram_a = gram_of(0)
    right_b = right_of(1)
    arrive(right_a)
    each(0, tile_roots, many)
    arrive(left_b)
    owner_grams(1)
    gram_b = gram_of(1)
    arrive(gram_a)
    each(0, finish_core, many)
    pack(0)
    mix_a = mix_of(0)
    each(0, right_out, many)
    arrive(right_b)
    each(1, tile_roots, many)
    arrive(gram_b)
    each(1, finish_core, many)
    pack(1)
    mix_b = mix_of(1)
    each(1, right_out, many)
    for j in range(slots):
        o = lax.div(mine[0, j], tiles)
        first = tab[at_source + o] == j
        out_right[j] = made_right[tab[at_seq + o] + jnp.where(first, 0, pairs)]
    sent(right_a)
    sent(right_b)
    arrive(mix_a)
    new_left(0)
    arrive(mix_b)
    new_left(1)
    keep_tiles()
    scale_rows()
    for moved in (routes, left_a, left_b, gram_a, gram_b, mix_a, mix_b):
        sent(moved)


def sweep(packed, own_left, own_right, add_left, add_right, n, m):
    tiles, order, half = own_left.shape
    slots = add_left.shape[0]
    wide = 2 * half
    vmem = pl.BlockSpec(memory_space=pltpu.VMEM)
    hbm = pl.BlockSpec(memory_space=pl.ANY)
    entries = 5 * CAP * n + 5 * slots + 2 * tiles
    return pl.pallas_call(
        functools.partial(sweep_kernel, n, m),
        in_specs=[pl.BlockSpec(memory_space=pltpu.SMEM), vmem] + [hbm] * 4,
        out_specs=[vmem] * 3,
        out_shape=[
            jax.ShapeDtypeStruct((tiles, order, half), BF16),
            jax.ShapeDtypeStruct((slots, order, half), BF16),
            jax.ShapeDtypeStruct((BR, order), F32),
        ],
        scratch_shapes=[
            pltpu.VMEM((tiles, order, half), BF16),
            pltpu.VMEM((tiles, order, half), BF16),
            pltpu.VMEM((slots, order, half), BF16),
            pltpu.VMEM((slots, order, half), BF16),
            pltpu.VMEM((CAP, n, order, half), BF16),
            pltpu.VMEM((CAP, n, order, half), BF16),
            pltpu.VMEM((CAP, n, order, half), BF16),
            pltpu.VMEM((n, order, half), BF16),
            pltpu.VMEM((n, order, half), BF16),
            pltpu.VMEM((CAP, n, half, wide), BF16),
            pltpu.VMEM((n, half, wide), BF16),
            pltpu.VMEM((n, half, wide), BF16),
            pltpu.VMEM((slots, wide, wide), F32),
            pltpu.VMEM((slots, wide, wide), F32),
            pltpu.VMEM((slots, wide, half), BF16),
            pltpu.VMEM((CAP, n, wide, half), BF16),
            pltpu.VMEM((CAP, n, wide, half), BF16),
            pltpu.VMEM((slots, order, half), BF16),
            pltpu.VMEM((BR, order, half), F32),
            pltpu.VMEM((2, BR, order), F32),
            pltpu.VMEM((n, BR, order), F32),
            pltpu.VMEM((2, 8, 128), F32),
            pltpu.VMEM((m, 8, 128), F32),
            pltpu.VMEM((n,) + packed.shape, jnp.int32),
            pltpu.SMEM((n,) + packed.shape, jnp.int32),
            pltpu.SMEM((entries,), jnp.int32),
            pltpu.SemaphoreType.DMA((10, n)),
            pltpu.SemaphoreType.DMA((10, n)),
            pltpu.SemaphoreType.DMA((2, m)),
            pltpu.SemaphoreType.DMA((11, 4)),
        ],
        compiler_params=pltpu.CompilerParams(
            collective_id=0, has_side_effects=True, vmem_limit_bytes=62 * 1024 * 1024
        ),
        name="sweep",
    )(packed, packed, own_left, own_right, add_left, add_right)


def local(
    current_left,
    current_right,
    current_rank,
    target_rank,
    update_left,
    update_right,
    update_rank,
    owner_slot,
):
    packed = jnp.concatenate([owner_slot, current_rank, target_rank, update_rank], axis=1)
    width = -(-packed.shape[1] // 128) * 128
    packed = jnp.pad(packed, ((0, 0), (0, width - packed.shape[1])))
    kept, right, scale = sweep(
        packed,
        current_left[0],
        current_right[0],
        update_left[0],
        update_right[0],
        lax.axis_size("col"),
        lax.axis_size("row"),
    )
    return (kept[None], right[None], scale)


def solution(mesh):
    return jax.shard_map(
        local,
        mesh=mesh,
        in_specs=(
            P("row", "col", None, None),
            P("row", "col", None, None),
            P("row", "col"),
            P("row", "col"),
            P("row", "col", None, None),
            P("row", "col", None, None),
            P("row", "col"),
            P("row", "col"),
        ),
        out_specs=(P("row", "col", None, None), P("row", "col", None, None), P("row", None)),
        check_vma=False,
    )
```

time: 263 us -> 224 us (0.85)
  Pallas kernels: 238 us -> 217 us
  other arithmetic: 9.74 us -> 0.78 us
  local copies, waits for them, and re-layouts: 13.7 us -> 6.24 us
    pallas_call x4 -> x1, Pallas kernels: 238 us -> 217 us  [sweep(): pl.pallas_call(functools.partial(sweep_kernel, n, m), in_specs=[pl.BlockS...]
    gather x3 -> x0, local copies, waits for them, and re-layouts: 9.97 us -> none  [take(): return jnp.take(values, index, axis=0, mode='clip')]
    unnamed x3 -> x7, local copies, waits for them, and re-layouts: 1.3 us -> 5.72 us
where the time goes in v3:
time: 224 us
  Pallas kernels  217 us (97%)
  local copies, waits for them, and re-layouts  6.24 us (3%)
    pallas_call x1, Pallas kernels, sweep(): pl.pallas_call(functools.partial(sweep_kernel, n, m), in_specs=[pl.BlockS...  217 us
    unnamed x7, local copies, waits for them, and re-layouts  5.72 us

profile of v3, /device:TPU:0, one launch (start us, length us, event | category | flops | bytes accessed | tf_op | source)
XLA Modules:
  0.0 224.3 jit_solution(16920545500903968535)
XLA Ops:
  0.6 0.8 pad_add_fusion
  1.4 0.5 pad.4.mine.packed
  1.9 216.6 %sweep.1 = (bf16[16,768,128]{2,1,0:T(8,128)(2,1)}, bf16[8,768,128]{2,1,0:T(8,128)(2,1)}, f32[2,768]{1,0:T(2,128)}) custom-call(s32[1,128]{1,0:T(1,128)} %pad.4.mine.packed, s32[1,128]{1,0:T(1,128)} %pad.4.mine.packed, bf16[16,768,128]{2,1,0:T(8,128)(2,1)} %bitcast.6, bf16[16,768,128]{2,1,0:T(8,128)(2,1)} %bitcast.7, bf16[8,768,128]{2,1,0:T(8,128)(2,1)} %bitcast.9, ...), custom_call_target="tpu_custom_call" | custom-call | tf_op jit(solution)/shard_map/sweep/pallas_call | solution.py:466
  218.6 0.0 copy-start
  218.6 4.0 %copy.14 = bf16[1,16,768,128]{3,2,1,0:T(8,128)(2,1)} copy(bf16[1,16,768,128]{3,2,1,0:T(8,128)(2,1)} %bitcast.8) | data formatting | bytes 6291456
  222.6 0.0 copy-done
  222.6 0.0 copy-start.1
  222.6 1.1 copy.15
  223.7 0.0 copy-done.1
  223.7 0.6 copy.16
Async XLA Ops:
  218.6 4.0 %copy-start = (bf16[8,768,128]{2,1,0:T(8,128)(2,1)S(1)}, bf16[8,768,128]{2,1,0:T(8,128)(2,1)}, u32[]{:S(2)}) copy-start(bf16[8,768,128]{2,1,0:T(8,128)(2,1)} %get-tuple-element.7) | copy-start | bytes 4718596
  222.6 1.1 copy-start.1

commit v4 on v3

--- a/solution.py
+++ b/solution.py
@@ -11,6 +11,7 @@
 CAP = 2
 BR = 2
 SWEEPS = 8
+FINE = 2
 ROOTS = 3
 F32 = jnp.float32
 BF16 = jnp.bfloat16
@@ -153,23 +154,36 @@
     pack_left(1)
     pl.semaphore_wait(barrier, n + m - 2)
 
-    def exchange(kind, src, dst):
-        copies = []
-        for step in [s for g in range(1, n // 2 + 1) for s in sorted({g, n - g})]:
-            peer = lax.rem(me + step, n)
-            copy = pltpu.make_async_remote_copy(
-                src_ref=src(peer),
-                dst_ref=dst(me),
-                send_sem=sends.at[kind, step],
-                recv_sem=recvs.at[kind, step],
-                device_id=(row, peer),
-                device_id_type=pl.DeviceIdType.MESH,
-            )
-            copy.start()
-            copies.append(copy)
+    steps = [s for g in range(1, n // 2 + 1) for s in sorted({g, n - g})]
+
+    def to_peer(kind, src, dst, step):
+        peer = lax.rem(me + step, n)
+        copy = pltpu.make_async_remote_copy(
+            src_ref=src(peer),
+            dst_ref=dst(me),
+            send_sem=sends.at[kind, step],
+            recv_sem=recvs.at[kind, step],
+            device_id=(row, peer),
+            device_id_type=pl.DeviceIdType.MESH,
+        )
+        copy.start()
+        return copy
+
+    def to_self(kind, src, dst):
         own = pltpu.make_async_copy(src(me), dst(me), locals_.at[kind, 0])
         own.start()
-        return own, copies
+        return own
+
+    def exchange(kind, src, dst):
+        copies = [to_peer(kind, src, dst, step) for step in steps]
+        return to_self(kind, src, dst), copies
+
+    def as_it_arrives(moved, work):
+        moved[0].wait()
+        work(me)
+        for step, copy in zip(steps, moved[1]):
+            copy.wait_recv()
+            work(lax.rem(me + n - step, n))
 
     def arrive(moved):
         moved[0].wait()
@@ -188,9 +202,6 @@
 
     def right_of(c):
         return exchange(2 + c, lambda p: send_right.at[c, p], lambda p: got_right[c].at[p])
-
-    def gram_of(c):
-        return exchange(4 + c, lambda p: gram_send.at[c, p], lambda p: got_gram[c].at[p])
 
     def mix_of(c):
         return exchange(6 + c, lambda p: mix_send.at[c, p], lambda p: got_mix.at[c, p])
@@ -203,14 +214,26 @@
             keeps.append(((i < half) & (i < cur)) | ((i >= half) & (i - half < add)))
         return keeps[0] & keeps[1], keeps[0]
 
-    def owner_grams(c):
-        def one(d, _):
-            cur = own_left[tab[at_tile + c * n + d]]
-            both = jnp.concatenate([cur, got_left[c, d]], axis=1)
-            gram_send[c, d] = contract_rows(cur, both).astype(BF16)
-            return 0
-
-        lax.fori_loop(0, n, one, 0)
+    def one_gram(c, d):
+        cur = own_left[tab[at_tile + c * n + d]]
+        both = jnp.concatenate([cur, got_left[c, d]], axis=1)
+        gram_send[c, d] = contract_rows(cur, both).astype(BF16)
+
+    def owner_grams(c, moved):
+        src, dst = (lambda p: gram_send.at[c, p]), (lambda p: got_gram[c].at[p])
+        copies = []
+        moved[0].wait()
+        one_gram(c, me)
+        own = to_self(4 + c, src, dst)
+        before = None
+        for step, copy in zip(steps, moved[1]):
+            copy.wait_recv()
+            one_gram(c, lax.rem(me + n - step, n))
+            if before is not None:
+                copies.append(to_peer(4 + c, src, dst, n - before))
+            before = step
+        copies.append(to_peer(4 + c, src, dst, n - before))
+        return own, copies
 
     def right_stack(c, k):
         at = c * pairs + k
@@ -250,10 +273,15 @@
         folded = root[:, :half] + root[:, half:]
         core = product(s, split(product(split(gram), split(folded))))
         y = core * lax.rsqrt(total(core * core) + 1e-06)
-        for _ in range(SWEEPS):
-            ys = split(y)
-            inner = product(ys, ys, (((0,), (0,)), ((), ())))
-            y = 1.5 * y - 0.5 * product(ys, split(inner))
+        for i in range(SWEEPS):
+            if i < SWEEPS - FINE:
+                upper = y.astype(BF16)
+                inner = contract_rows(upper, upper).astype(BF16)
+                y = 1.5 * y - 0.5 * jnp.dot(upper, inner, preferred_element_type=F32)
+            else:
+                ys = split(y)
+                inner = product(ys, ys, (((0,), (0,)), ((), ())))
+                y = 1.5 * y - 0.5 * product(ys, split(inner))
         y = split(jnp.where(iota(y.shape, 1) < tab[at_keep + at], y, 0.0))
         mixes[at] = product(s, y).astype(BF16)
         mix = product(split(inverses[at]), y) * math.sqrt(order)
@@ -339,13 +367,12 @@
     fresh = send_right
 
     def new_left(c):
-        def one(d, _):
+        def one(d):
             both = jnp.concatenate([own_left[tab[at_tile + c * n + d]], got_left[c, d]], axis=1)
             made = jnp.dot(both, got_mix[c, d], preferred_element_type=F32)
             fresh[c, d] = made.astype(BF16)
-            return 0
-
-        lax.fori_loop(0, n, one, 0)
+
+        return one
 
     def keep_tiles():
         squares[...] = jnp.zeros_like(squares)
@@ -414,27 +441,26 @@
     loads[1].wait()
     pack_right()
     right_a = right_of(0)
-    left_b = left_of(1)
     index_tables()
     arrival_tables()
     loads[2].wait()
     loads[3].wait()
-    arrive(left_a)
-    owner_grams(0)
-    gram_a = gram_of(0)
+    gram_a = owner_grams(0, left_a)
     right_b = right_of(1)
     arrive(right_a)
     each(0, tile_roots, many)
-    arrive(left_b)
-    owner_grams(1)
-    gram_b = gram_of(1)
     arrive(gram_a)
     each(0, finish_core, many)
     pack(0)
     mix_a = mix_of(0)
+    left_b = left_of(1)
     each(0, right_out, many)
     arrive(right_b)
     each(1, tile_roots, many)
+    sent(right_a)
+    sent(right_b)
+    as_it_arrives(mix_a, new_left(0))
+    gram_b = owner_grams(1, left_b)
     arrive(gram_b)
     each(1, finish_core, many)
     pack(1)
@@ -444,12 +470,7 @@
         o = lax.div(mine[0, j], tiles)
         first = tab[at_source + o] == j
         out_right[j] = made_right[tab[at_seq + o] + jnp.where(first, 0, pairs)]
-    sent(right_a)
-    sent(right_b)
-    arrive(mix_a)
-    new_left(0)
-    arrive(mix_b)
-    new_left(1)
+    as_it_arrives(mix_b, new_left(1))
     keep_tiles()
     scale_rows()
     for moved in (routes, left_a, left_b, gram_a, gram_b, mix_a, mix_b):

time: 224 us -> 225 us (level)
  no operation moved by 1% of the time
where the time goes in v4:
time: 225 us
  Pallas kernels  218 us (97%)
  local copies, waits for them, and re-layouts  6.24 us (3%)
    pallas_call x1, Pallas kernels, sweep(): pl.pallas_call(functools.partial(sweep_kernel, n, m), in_specs=[pl.BlockS...  218 us
    unnamed x7, local copies, waits for them, and re-layouts  5.72 us

profile of v4, /device:TPU:0, one launch (start us, length us, event | category | flops | bytes accessed | tf_op | source)
XLA Modules:
  0.0 225.3 jit_solution(78075578211227981)
XLA Ops:
  0.6 0.8 pad_add_fusion
  1.4 0.5 pad.4.mine.packed
  1.9 217.6 %sweep.1 = (bf16[16,768,128]{2,1,0:T(8,128)(2,1)}, bf16[8,768,128]{2,1,0:T(8,128)(2,1)}, f32[2,768]{1,0:T(2,128)}) custom-call(s32[1,128]{1,0:T(1,128)} %pad.4.mine.packed, s32[1,128]{1,0:T(1,128)} %pad.4.mine.packed, bf16[16,768,128]{2,1,0:T(8,128)(2,1)} %bitcast.6, bf16[16,768,128]{2,1,0:T(8,128)(2,1)} %bitcast.7, bf16[8,768,128]{2,1,0:T(8,128)(2,1)} %bitcast.9, ...), custom_call_target="tpu_custom_call" | custom-call | tf_op jit(solution)/shard_map/sweep/pallas_call | solution.py:487
  219.6 0.0 copy-start
  219.6 4.0 %copy.14 = bf16[1,16,768,128]{3,2,1,0:T(8,128)(2,1)} copy(bf16[1,16,768,128]{3,2,1,0:T(8,128)(2,1)} %bitcast.8) | data formatting | bytes 6291456
  223.6 0.0 copy-done
  223.6 0.0 copy-start.1
  223.6 1.1 copy.15
  224.7 0.0 copy-done.1
  224.7 0.6 copy.16
Async XLA Ops:
  219.6 4.0 %copy-start = (bf16[8,768,128]{2,1,0:T(8,128)(2,1)S(1)}, bf16[8,768,128]{2,1,0:T(8,128)(2,1)}, u32[]{:S(2)}) copy-start(bf16[8,768,128]{2,1,0:T(8,128)(2,1)} %get-tuple-element.7) | copy-start | bytes 4718596
  223.6 1.1 copy-start.1
